TPU v7x, 32 devices: a whole 2x2x4 slice. The times are simulated.
32 devices in a mesh: jet: 8 (over z, y), grp: 4 (over x, core).
Axes of the slice: x: 2, y: 2, z: 4, core: 2. Of those that a mesh axis runs over, the one named last changes fastest.
Arguments:
- sources: float32 [3, 24, 192, 384], P(None, 'jet', 'grp'), may hold values from -8 to 8
- cotangent: float32 [3, 24, 192, 384], P(None, 'jet', 'grp'), may hold values from -6 to 6
- width_class: int32 [24, 192, 3], P('jet', 'grp'), may hold values from 0 to 7
Outputs:
- filtered: float32 [3, 24, 192, 384], P(None, 'jet', 'grp')
- adjoint: float32 [3, 24, 192, 384], P(None, 'jet', 'grp')
All inputs are finite; a program needn't handle non-finite values.
Results may differ from a plain program's by a relative error of at most 0.00002.
Values sent between devices are 32-bit elements; how exact they have to be, the bound alone decides.
No kernel may reach another device: no remote copies, remote signals or barrier semaphores. Data moves between devices by JAX's collectives and lax.ppermute only.
A program may use at most 128 MiB of HBM per device.

v0:
```python
import functools

import jax
import jax.numpy as jnp
from jax import lax
from jax.experimental import pallas as pl
from jax.experimental.pallas import tpu as pltpu
from jax.sharding import PartitionSpec as P


BLOCK = 128
CLASSES = 8
COARSE_SWEEPS = 8
DEEP = 3
O = 16
LO = 8
WIDTH_TABLE = (2.5, 3.5, 4.5, 5.0, 6.0, 7.0, 8.5, 10.0)
RELAXATION = 0.8
COARSE_RELAX = 0.8
F32 = jnp.float32
BF16 = jnp.bfloat16


VM = pl.BlockSpec(memory_space=pltpu.VMEM)
SM = pl.BlockSpec(memory_space=pltpu.SMEM)


def padded(shape):
    n = 4
    for d in shape[:-2]:
        n *= d
    return n * (-(-shape[-2] // 8) * 8) * (-(-shape[-1] // BLOCK) * BLOCK)


def call(kernel, outs, scratch, *args, smem=0, cost=(1000000, 1000000)):
    specs = [SM] * smem + [VM] * (len(args) - smem)
    need = sum(map(padded, scratch))
    return pl.pallas_call(
        kernel,
        out_shape=[jax.ShapeDtypeStruct(s, F32) for s in outs],
        in_specs=specs,
        out_specs=[VM] * len(outs),
        scratch_shapes=[pltpu.VMEM(s, F32) for s in scratch],
        cost_estimate=pl.CostEstimate(flops=cost[0], bytes_accessed=cost[1], transcendentals=0),
        compiler_params=pltpu.CompilerParams(vmem_limit_bytes=need + (6 << 20)),
    )(*args)


def iota(shape, dim):
    return lax.broadcasted_iota(jnp.int32, shape, dim)


def pack_x(info, f, g, ks, to_a, to_b):
    nf, nz, nx, ny = f.shape
    even = info[6] == 0
    kr = kappa_row(nf, nz)

    def put(at, rows, first, last):
        to_a[at:at + rows, 0:last.shape[1]] = jnp.where(even, last, first)
        to_b[at:at + rows, 0:last.shape[1]] = jnp.where(even, first, last)

    for s, ref in enumerate((f, g)):
        for a in range(nf):
            for p in range(nz):
                put(((s * nf + a) * nz + p) * DEEP, DEEP, ref[a, p, 0:DEEP, :], ref[a, p, nx - DEEP:nx, :])
    for ref in (to_a, to_b):
        ref[kr:kr + 8, :] = jnp.zeros((8, ny), F32)
    put(kr, 4, ks[0:4, :], ks[nx - 4:nx, :])


def kappa_row(nf, nz):
    return -(-2 * nf * nz * DEEP // 8) * 8


def pack_y(info, xa, xb, ks, out, low, high, *, nf, nz, nx):
    even = info[6] == 0
    low[...] = jnp.where(even, xb[...], xa[...])
    high[...] = jnp.where(even, xa[...], xb[...])
    for a in range(2 * nf):
        for p in range(nz):
            src = (a * nz + p) * DEEP
            at = (a * nz + p) * 4
            out[at:at + 2, :] = low[src + 1:src + 3, :]
            out[at + 2:at + 4, :] = high[src:src + 2, :]
    kr = kappa_row(nf, nz)
    at = 8 * nf * nz
    out[at:at + nx // 2, 0:BLOCK] = ks[0:nx // 2, :]
    out[at:at + nx // 2, BLOCK:2 * BLOCK] = ks[nx // 2:nx, :]
    out[at:at + 4, 2 * BLOCK:3 * BLOCK] = low[kr:kr + 4, 0:BLOCK]
    out[at + 4:at + 8, 2 * BLOCK:3 * BLOCK] = high[kr:kr + 4, 0:BLOCK]
    out[at + 8:at + nx // 2, 2 * BLOCK:3 * BLOCK] = jnp.zeros((nx // 2 - 8, BLOCK), F32)


def columns_of(pack, at, nx):
    half = nx // 2
    return (
        (O - 4, pack[at:at + 4, 2 * BLOCK:3 * BLOCK]),
        (O, pack[at:at + half, 0:BLOCK]),
        (O + half, pack[at:at + half, BLOCK:2 * BLOCK]),
        (O + nx, pack[at + 4:at + 8, 2 * BLOCK:3 * BLOCK]),
    )


def dot01(x, m):
    h = x.astype(BF16)
    r = x - h.astype(F32)
    i = r.astype(BF16)
    j = (r - i.astype(F32)).astype(BF16)
    dot = functools.partial(jnp.dot, preferred_element_type=F32)
    return dot(h, m) + dot(i, m) + dot(j, m)


def lane_sum(b):
    l, m = iota((BLOCK, BLOCK), 0), iota((BLOCK, BLOCK), 1)
    return jnp.where((l + b * BLOCK) // 4 == m, 1.0 / 16.0, 0.0).astype(BF16)


def lane_copy(ny):
    m, l = iota((BLOCK, ny), 0), iota((BLOCK, ny), 1)
    return jnp.where(l // 4 == m, 1.0, 0.0).astype(BF16)


def around(v, nb, lane):
    rl = [pltpu.roll(x, 1, 1) for x in v]
    rr = [pltpu.roll(x, BLOCK - 1, 1) for x in v]
    left = [jnp.where(lane == 0, rl[i - 1] if i > 0 else 0.0, rl[i]) for i in range(nb)]
    right = [jnp.where(lane == BLOCK - 1, rr[i + 1] if i < nb - 1 else 0.0, rr[i]) for i in range(nb)]
    return left, right


def pull(src, co, p, r, a, nb, lane):
    czm, czp, cxm, cxp, cym, cyp = co
    v = [src[a, p, b, r:r + 8, :] for b in range(nb)]
    left, right = around(v, nb, lane)
    out = []
    for b in range(nb):
        s = czm[b] * src[a, p - 1, b, r:r + 8, :] + czp[b] * src[a, p + 1, b, r:r + 8, :]
        s = s + cxm[b] * src[a, p, b, r - 1:r + 7, :] + cxp[b] * src[a, p, b, r + 1:r + 9, :]
        s = s + cym[b] * left[b] + cyp[b] * right[b]
        out.append(s)
    return v, out


def coefs_at(coef, p, r, nb):
    cz, cx, cm, cp, _ = coef
    return (
        [cz[p, b, r:r + 8, :] for b in range(nb)],
        [cz[p + 1, b, r:r + 8, :] for b in range(nb)],
        [cx[p, b, r - 1:r + 7, :] for b in range(nb)],
        [cx[p, b, r:r + 8, :] for b in range(nb)],
        [cm[p, b, r:r + 8, :] for b in range(nb)],
        [cp[p, b, r:r + 8, :] for b in range(nb)],
    )


def rows_of(wide, nx):
    return range(LO, LO + nx + 16, 8) if wide else range(O, O + nx, 8)


def sweep(dst, src, rhs, coef, first, count, stride, wide, nx):
    inv = coef[4]
    nf, nb = src.shape[0], src.shape[2]
    lane = iota((8, BLOCK), 1)

    def plane(i, _):
        p = first + i * stride
        for r in rows_of(wide, nx):
            co = coefs_at(coef, p, r, nb)
            w = [inv[p, b, r:r + 8, :] for b in range(nb)]
            for a in range(nf):
                v, s = pull(src, co, p, r, a, nb, lane)
                for b in range(nb):
                    dst[a, p, b, r:r + 8, :] = (1.0 - RELAXATION) * v[b] + w[b] * (rhs[a, p, b, r:r + 8, :] + s[b])
        return 0

    lax.fori_loop(0, count, plane, 0)


def three(ua, ub, rhs, coef, nz, nx):
    sweep(ub, ua, rhs, coef, 2, 2 * nz - 1, 1, True, nx)
    sweep(ub, ua, rhs, coef, 1, 2, 3 * nz - 3, False, nx)
    sweep(ua, ub, rhs, coef, nz, nz, 1, True, nx)
    sweep(ua, ub, rhs, coef, nz - 1, 2, nz + 1, False, nx)


def final(dst, src, rhs, coef, nz, nx):
    inv = coef[4]
    nf, nb = src.shape[0], src.shape[2]
    lane = iota((8, BLOCK), 1)

    def plane(i, _):
        p = nz + i
        for r in rows_of(False, nx):
            co = coefs_at(coef, p, r, nb)
            w = [inv[p, b, r:r + 8, :] for b in range(nb)]
            for a in range(nf):
                v, s = pull(src, co, p, r, a, nb, lane)
                for b in range(nb):
                    c = slice(b * BLOCK, (b + 1) * BLOCK)
                    q = r - O
                    dst[a, i, q:q + 8, c] = (1.0 - RELAXATION) * v[b] + w[b] * (rhs[a, i, q:q + 8, c] + s[b])
        return 0

    lax.fori_loop(0, nz, plane, 0)


def restrict_residual(out, base, src, rhs, coef, diag, tmp, parts, nz, nx):
    nf, nb = src.shape[0], src.shape[2]
    lane = iota((8, BLOCK), 1)

    def plane(i, _):
        p = nz + i
        for r in rows_of(False, nx):
            co = coefs_at(coef, p, r, nb)
            d = [diag[i, b, r:r + 8, :] for b in range(nb)]
            for a in range(nf):
                v, s = pull(src, co, p, r, a, nb, lane)
                for b in range(nb):
                    c = slice(b * BLOCK, (b + 1) * BLOCK)
                    q = r - O
                    tmp[b, a * nz + i, q:q + 8, :] = rhs[a, i, q:q + 8, c] - d[b] * v[b] + s[b]
        return 0

    lax.fori_loop(0, nz, plane, 0)
    nc = nx // 4
    total = None
    for b in range(nb):
        for k in range(nf * nz):
            parts[k * nc:(k + 1) * nc, :] = sum(tmp[b, k, pl.ds(j, nc, stride=4), :] for j in range(4))
        dot = dot01(parts[...], lane_sum(b))
        total = dot if total is None else total + dot
    out[base:base + total.shape[0], :] = total


def coarse_kappa(out, ks, tmp, nz, nx, nb):
    nc = nx // 4
    tmp[0, 0, 0:nx, :] = ks[...]
    kc = sum(tmp[0, 0, pl.ds(j, nc, stride=4), :] for j in range(4)) * (1.0 / 64.0)
    for p in range(nz):
        l, m = iota((BLOCK, BLOCK), 0), iota((BLOCK, BLOCK), 1)
        pick = jnp.where((l - p * nb == m - (BLOCK - nb)) & (m >= BLOCK - nb), 1.0, 0.0).astype(BF16)
        rows = slice(p * nc, (p + 1) * nc)
        out[rows, :] = out[rows, :] + dot01(kc, pick)


def coefficients(info, ka, kb, own, partner, other, cz, cx, cm, cp, inv, diag, kap, *, nz, nx, nb, at):
    first_j, last_j, first_g, last_g = (info[i] for i in range(1, 5))
    pbase = jnp.where(info[0] == 0, 1 + 2 * nz, 1)
    for base, ref in ((pbase, partner), (2 + 2 * nz - pbase, other), (1 + nz, own)):
        for row, value in columns_of(ref, at, nx):
            n = value.shape[0]
            for p in range(nz):
                for b in range(nb):
                    c = p * nb + b
                    kap[base + p, b, row:row + n, :] = jnp.broadcast_to(value[:, c:c + 1], (n, BLOCK))
    lo2 = jnp.where(info[7] == 0, kb[...], ka[...])
    hi2 = jnp.where(info[7] == 0, ka[...], kb[...])
    for b in range(nb):
        c = (nz - 1) * nb + b
        kap[0, b, O:O + nx, :] = jnp.broadcast_to(lo2[:, c:c + 1], (nx, BLOCK))
        kap[3 * nz + 1, b, O:O + nx, :] = jnp.broadcast_to(hi2[:, b:b + 1], (nx, BLOCK))
    lane = iota((8, BLOCK), 1)

    def cplane(p, _):
        out = ((first_j == 1) & (p < nz)) | ((last_j == 1) & (p >= 2 * nz))
        for r in rows_of(True, nx):
            row = iota((8, BLOCK), 0) + (r - O)
            here = jnp.where(((row < 0) & (first_g == 1)) | ((row >= nx) & (last_g == 1)) | out, 0.0, RELAXATION)
            s8 = slice(r, r + 8)
            k = [kap[p + 1, b, s8, :] for b in range(nb)]
            for b in range(nb):
                zm = 0.5 * (kap[p, b, s8, :] + k[b])
                zp = 0.5 * (k[b] + kap[p + 2, b, s8, :])
                xp = 0.5 * (k[b] + kap[p + 1, b, r + 1:r + 9, :])
                xm = 0.5 * (k[b] + kap[p + 1, b, r - 1:r + 7, :])
                ym = jnp.where(lane == 0, 0.5 * (k[b] + k[b - 1]) if b > 0 else 0.5 * k[b], k[b])
                yp = jnp.where(lane == BLOCK - 1, 0.5 * (k[b] + k[b + 1]) if b < nb - 1 else 0.5 * k[b], k[b])
                cz[p, b, s8, :] = zm
                cz[p + 1, b, s8, :] = zp
                cx[p, b, s8, :] = xp
                cm[p, b, s8, :] = ym
                cp[p, b, s8, :] = yp
                d = 1.0 + zm + zp + xm + xp + ym + yp
                inv[p, b, s8, :] = here / d

                @pl.when((p >= nz) & (p < 2 * nz))
                def _():
                    diag[p - nz, b, s8, :] = d
        return 0

    lax.fori_loop(0, 3 * nz, cplane, 0)


def lay(dst, ref, a, p, q, rows, lo_row, hi_row, nx, nb):
    width, _, pack = rows
    for b in range(nb):
        c = slice(b * BLOCK, (b + 1) * BLOCK)
        dst[a, q, b, O:O + nx, :] = ref[a, p, :, c]
        if pack is not None:
            dst[a, q, b, O - width:O, :] = pack[0][lo_row:lo_row + width, c]
            dst[a, q, b, O + nx:O + nx + width, :] = pack[1][hi_row:hi_row + width, c]


def ends(low, high, s, a, p, nf, nz):
    at = ((s * nf + a) * nz + p) * DEEP
    return (DEEP, None, (low, high)), at, at


def corners(pack, s, a, p, nf, nz):
    at = ((s * nf + a) * nz + p) * 4
    return (2, None, (pack, pack)), at, at + 2


def start(dst, own, inv, p, nx, nb, nf):
    for a in range(nf):
        for b in range(nb):
            for r in rows_of(True, nx):
                dst[a, p, b, r:r + 8, :] = inv[p, b, r:r + 8, :] * own[a, p, b, r:r + 8, :]


def fwd_before(info, f, pf, rf, low, high, py, ry, ks, cz, cx, cm, cp, inv, diag, u3, rc, fx, ub, tmp, parts):
    nf, nz, nx, ny = f.shape
    nb = ny // BLOCK
    par = info[0]
    pbase = jnp.where(par == 0, 2 * nz, 0)
    rbase = 2 * nz - pbase
    for a in range(nf):
        for p in range(nz):
            lay(fx, f, a, p, nz + p, *ends(low, high, 0, a, p, nf, nz), nx, nb)
            lay(fx, pf, a, p, pbase + p, *corners(py, 0, a, p, nf, nz), nx, nb)
            lay(fx, rf, a, p, rbase + p, *corners(ry, 0, a, p, nf, nz), nx, nb)
    coef = (cz, cx, cm, cp, inv)

    def one(p, _):
        start(u3, fx, inv, p, nx, nb, nf)
        return 0

    lax.fori_loop(0, 3 * nz, one, 0)
    three(u3, ub, fx, coef, nz, nx)
    restrict_residual(rc, 0, u3, f, coef, diag, tmp, parts, nz, nx)
    coarse_kappa(rc, ks, tmp, nz, nx, nb)


def adj_before(info, g, pg, rn, low, high, rcf, cz, cx, cm, cp, inv, diag, rc, gx, ua, tmp, parts):
    nf, nz, nx, ny = g.shape
    nb = ny // BLOCK
    par = info[0]
    pp = jnp.where(par == 0, 2 * nz, nz - 1)
    rp = 3 * nz - 1 - pp
    near = jnp.where(par == 0, 0, nz - 1)
    none = (0, None, None)
    for a in range(nf):
        for p in range(nz):
            lay(gx, g, a, p, nz + p, *ends(low, high, 1, a, p, nf, nz), nx, nb)
        lay(gx, pg, a, near, pp, none, 0, 0, nx, nb)
        lay(gx, rn, a, 0, rp, none, 0, 0, nx, nb)

    def one(p, _):
        start(ua, gx, inv, p, nx, nb, nf)
        return 0

    lax.fori_loop(nz - 1, 2 * nz + 1, one, 0)
    n = rcf.shape[0]
    rc[0:n, :] = rcf[...]
    restrict_residual(rc, n, ua, g, (cz, cx, cm, cp, inv), diag, tmp, parts, nz, nx)


def prolong(dst, e, k, a, q, nx, nb):
    nc = nx // 4
    for b in range(nb):
        part = e[k * 16:k * 16 + nc + 2, b * BLOCK:(b + 1) * BLOCK]
        for j in range(4):
            dst[a, q, b, pl.ds(O - 4 + j, nc + 2, stride=4), :] = part


def fwd_after(info, f, u3, cz, cx, cm, cp, inv, est, ea, eb, filtered, ua, e):
    nf, nz, nx, ny = f.shape
    nb = ny // BLOCK
    copy = lane_copy(ny)
    coef = (cz, cx, cm, cp, inv)
    qa = jnp.where(info[0] == 0, 2 * nz, nz - 1)
    for ref, slots, base in ((est, nz, nz), (ea, 1, qa), (eb, 1, 3 * nz - 1 - qa)):
        n = nf * slots * 16
        e[0:n, :] = dot01(ref[0:n, :], copy)
        for a in range(nf):
            for i in range(slots):
                prolong(ua, e, a * slots + i, a, base + i, nx, nb)

    def one(p, _):
        for a in range(nf):
            for b in range(nb):
                for r in rows_of(True, nx):
                    ua[a, p, b, r:r + 8, :] = ua[a, p, b, r:r + 8, :] + u3[a, p, b, r:r + 8, :]
        return 0

    lax.fori_loop(nz - 1, 2 * nz + 1, one, 0)
    final(filtered, ua, f, coef, nz, nx)


def adj_after(info, g, pg, rn, rr, low, high, py, ry, cz, cx, cm, cp, inv, est, ea, eb, adjoint, gx, ua, ub, e):
    nf, nz, nx, ny = g.shape
    nb = ny // BLOCK
    par = info[0]
    pbase = jnp.where(par == 0, 2 * nz, 0)
    rbase = 2 * nz - pbase
    near = jnp.where(par == 0, nz - 1, 0)
    rest = jnp.where(par == 0, 0, 1)
    for a in range(nf):
        for p in range(nz):
            lay(gx, g, a, p, nz + p, *ends(low, high, 1, a, p, nf, nz), nx, nb)
            lay(gx, pg, a, p, pbase + p, *corners(py, 1, a, p, nf, nz), nx, nb)
        lay(gx, rn, a, 0, rbase + near, (0, None, None), 0, 0, nx, nb)
        for p in range(nz - 1):
            lay(gx, rr, a, p, rbase + rest + p, (0, None, None), 0, 0, nx, nb)
        for p in range(nz):
            (width, _, pack), lo_row, hi_row = corners(ry, 1, a, p, nf, nz)
            for b in range(nb):
                c = slice(b * BLOCK, (b + 1) * BLOCK)
                gx[a, rbase + p, b, O - width:O, :] = ry[lo_row:lo_row + width, c]
                gx[a, rbase + p, b, O + nx:O + nx + width, :] = ry[hi_row:hi_row + width, c]
    copy = lane_copy(ny)
    coef = (cz, cx, cm, cp, inv)
    n = nf * nz * 16
    for ref, at, base in ((est, n, nz), (ea, nf * 16, pbase), (eb, nf * 16, rbase)):
        e[...] = dot01(ref[at:at + n, :], copy)
        for a in range(nf):
            for i in range(nz):
                prolong(ua, e, a * nz + i, a, base + i, nx, nb)

    def one(p, _):
        for b in range(nb):
            for r in rows_of(True, nx):
                w = inv[p, b, r:r + 8, :]
                for a in range(nf):
                    ua[a, p, b, r:r + 8, :] = ua[a, p, b, r:r + 8, :] + w * gx[a, p, b, r:r + 8, :]
        return 0

    lax.fori_loop(0, 3 * nz, one, 0)
    three(ua, ub, gx, coef, nz, nx)
    final(adjoint, ua, g, coef, nz, nx)


def coarse(info, rc, est, to_a, to_b, full, e0, e1, ck, cf, *, nf, nz, ng, nc, nb):
    half = nf
    nf = 2 * nf
    nr = ng * nc
    per = rc.shape[0] // ng
    lane = iota((8, BLOCK), 1)
    used = BLOCK // 4 * nb
    valid = lane < used
    zero = jnp.zeros((8, BLOCK), F32)
    for ref in (e0, e1, ck):
        for a in range(ref.shape[0]):
            ref[a, 0:8, :] = zero
            ref[a, 8 + nr:16 + nr, :] = zero
    at = info[5] * nc
    for k in range(nf * nz):
        for i in range(ng):
            row = i * per + (0 if k < half * nz else per // 2) + (k % (half * nz)) * nc
            full[k, i * nc:(i + 1) * nc, :] = rc[row:row + nc, :]
    for p in range(nz):
        for r in range(0, nr, 8):
            raw = full[p, r:r + 8, :]
            kc = zero
            for b in range(nb):
                column = jnp.broadcast_to(raw[:, BLOCK - nb + b:BLOCK - nb + b + 1], (8, BLOCK))
                kc = jnp.where(lane // (BLOCK // 4) == b, column, kc)
            ck[p, 8 + r:16 + r, :] = kc
            full[p, r:r + 8, :] = jnp.where(valid, raw, 0.0)
    for p in range(nz):
        dsum = zero
        rsum = [zero] * nf
        for r in range(0, nr, 8):
            s8 = slice(r, r + 8)
            k = ck[p, 8 + r:16 + r, :]
            xm = jnp.where(valid, 0.5 * (k + ck[p, 7 + r:15 + r, :]), 0.0)
            xp = jnp.where(valid, 0.5 * (k + ck[p, 9 + r:17 + r, :]), 0.0)
            ym = jnp.where(valid, 0.5 * (k + pltpu.roll(k, 1, 1)), 0.0)
            yp = jnp.where(valid, 0.5 * (k + pltpu.roll(k, BLOCK - 1, 1)), 0.0)
            d = 1.0 + xm + xp + ym + yp
            dsum = dsum + jnp.where(valid, d, 0.0)
            ci = jnp.where(valid, COARSE_RELAX / d, 0.0)
            cf[0, s8, :] = xm
            cf[1, s8, :] = xp
            cf[2, s8, :] = ym
            cf[3, s8, :] = yp
            cf[4, s8, :] = ci
            for a in range(nf):
                v = full[a * nz + p, s8, :]
                rsum[a] = rsum[a] + v
                e0[a, 8 + r:16 + r, :] = ci * v
        total = jnp.sum(dsum)
        shift = [jnp.sum(rsum[a]) / total for a in range(nf)]
        src, dst = e0, e1
        for n in range(COARSE_SWEEPS - 1):
            for r in range(0, nr, 8):
                s8 = slice(r, r + 8)
                c = [cf[i, s8, :] for i in range(5)]
                for a in range(nf):
                    v = src[a, 8 + r:16 + r, :]
                    s = c[0] * src[a, 7 + r:15 + r, :] + c[1] * src[a, 9 + r:17 + r, :]
                    s = s + c[2] * pltpu.roll(v, 1, 1) + c[3] * pltpu.roll(v, BLOCK - 1, 1)
                    v = (1.0 - COARSE_RELAX) * v + c[4] * (full[a * nz + p, s8, :] + s)
                    if n == COARSE_SWEEPS - 2:
                        v = jnp.where(valid, v + shift[a], 0.0)
                    dst[a, 8 + r:16 + r, :] = v
            src, dst = dst, src
        for a in range(nf):
            own = src[a, pl.ds(at + 7, 16), :]
            k = a * nz + p
            est[k * 16:(k + 1) * 16, :] = own
            if a >= half:
                m = (half + k - half * nz) * 16
                to_a[m:m + 16, :] = own
                to_b[m:m + 16, :] = own
            elif p in (0, nz - 1):
                m = slice(a * 16, (a + 1) * 16)

                @pl.when((info[0] == 0) == (p == nz - 1))
                def _():
                    to_a[m, :] = own

                @pl.when((info[0] == 0) == (p == 0))
                def _():
                    to_b[m, :] = own


def kappa_columns(width_class):
    table = jnp.array(WIDTH_TABLE, F32)
    table = table * table / 24.0
    hits = (width_class[..., None] == jnp.arange(CLASSES, dtype=jnp.int32)).astype(F32)
    kappa = jnp.sum(hits * table, axis=-1)
    nz, nx, nb = kappa.shape
    columns = jnp.transpose(kappa, (1, 0, 2)).reshape(nx, nz * nb)
    return jnp.pad(columns, ((0, 0), (0, BLOCK - nz * nb)))


def cycle(f, g, width_class):
    nf, nz, nx, ny = f.shape
    nb = ny // BLOCK
    nc = nx // 4
    nj, ng = lax.axis_size("jet"), lax.axis_size("grp")
    assert nz == DEEP and nj % 2 == 0
    j, gi = lax.axis_index("jet"), lax.axis_index("grp")
    par = j % 2
    zp = (j // 2) % 2
    info = jnp.stack([par, (j == 0) * 1, (j == nj - 1) * 1, (gi == 0) * 1, (gi == ng - 1) * 1, gi, gi % 2, zp]).astype(jnp.int32)

    def both(pairs):
        return [p for a, b in pairs for p in ((a, b), (b, a))]

    swap = both([(i, i + 1) for i in range(0, nj, 2)])
    side = both([(i, i + 1) for i in range(1, nj - 1, 2)])
    relay = [(i, i + 2) for i in range(0, nj - 2, 2)] + [(i, i - 2) for i in range(3, nj, 2)]
    two_a = both([(i, i + 2) for i in range(nj - 2) if (i // 2) % 2 == 0])
    two_b = both([(i, i + 2) for i in range(nj - 2) if (i // 2) % 2 == 1])
    x_a = both([(i, i + 1) for i in range(0, ng - 1, 2)])
    x_b = both([(i, i + 1) for i in range(1, ng - 1, 2)])

    pf = lax.ppermute(f, "jet", swap)
    ks = kappa_columns(width_class)
    ka, kb = lax.ppermute(ks, "jet", two_a), lax.ppermute(ks, "jet", two_b)
    xs = (kappa_row(nf, nz) + 8, ny)
    to_a, to_b = call(pack_x, [xs] * 2, [], info, f, g, ks, smem=1)
    xa, xb = lax.ppermute(to_a, "grp", x_a), lax.ppermute(to_b, "grp", x_b)
    krow = 8 * nf * nz
    ypack, low, high = call(functools.partial(pack_y, nf=nf, nz=nz, nx=nx), [(krow + nx // 2, ny), xs, xs], [], info, xa, xb, ks, smem=1)
    py = lax.ppermute(ypack, "jet", swap)
    ry = lax.ppermute(ypack, "jet", side)
    pg = lax.ppermute(g, "jet", swap)
    rf = lax.ppermute(pf, "jet", relay)
    near = lax.dynamic_slice_in_dim(pg, (1 - par) * (nz - 1), 1, 1)
    rest = lax.dynamic_slice_in_dim(pg, par, nz - 1, 1)
    rn = lax.ppermute(near, "jet", relay)
    rr = lax.ppermute(rest, "jet", relay)

    xr = nx + 32
    deep = (nf, 3 * nz, nb, xr, BLOCK)
    co = (3 * nz, nb, xr, BLOCK)
    coefs = call(
        functools.partial(coefficients, nz=nz, nx=nx, nb=nb, at=krow),
        [(3 * nz + 1, nb, xr, BLOCK), co, co, co, co, (nz, nb, xr, BLOCK)], [(3 * nz + 2, nb, xr, BLOCK)],
        info, ka, kb, ypack, py, ry, smem=1)
    coef, diag = coefs[:5], coefs[5]
    rows = -(-nf * nz * nc // 8) * 8
    scratch = [(nb, nf * nz, nx, BLOCK), (rows, BLOCK)]
    u3, rcf = call(fwd_before, [deep, (rows, BLOCK)], [deep, deep] + scratch, info, f, pf, rf, low, high, py, ry, ks, *coef, diag, smem=1)
    (rc,) = call(adj_before, [(2 * rows, BLOCK)], [deep, deep] + scratch, info, g, pg, rn, low, high, rcf, *coef, diag, smem=1)
    whole = lax.all_gather(rc, "grp", axis=0, tiled=True)
    nr = ng * nc
    solve = [(2 * nf * nz, nr, BLOCK), (2 * nf, nr + 16, BLOCK), (2 * nf, nr + 16, BLOCK), (nz, nr + 16, BLOCK), (5, nr, BLOCK)]
    sent = (nf * (nz + 1) * 16, BLOCK)
    est, to_a, to_b = call(
        functools.partial(coarse, nf=nf, nz=nz, ng=ng, nc=nc, nb=nb),
        [(2 * nf * nz * 16, BLOCK), sent, sent], solve, info, whole, smem=1)
    ea, eb = lax.ppermute(to_a, "jet", swap), lax.ppermute(to_b, "jet", side)
    (filtered,) = call(fwd_after, [f.shape], [deep, (nf * nz * 16, ny)], info, f, u3, *coef, est, ea, eb, smem=1)
    (adjoint,) = call(adj_after, [g.shape], [deep, deep, deep, (nf * nz * 16, ny)], info, g, pg, rn, rr, low, high, py, ry, *coef, est, ea, eb, smem=1)
    return filtered, adjoint


def solution(mesh):
    placed = (P(None, "jet", "grp", None), P(None, "jet", "grp", None), P("jet", "grp", None))
    return jax.shard_map(
        cycle,
        mesh=mesh,
        in_specs=placed,
        out_specs=(P(None, "jet", "grp", None), P(None, "jet", "grp", None)),
        check_vma=False,
    )
```

profile of v0, /device:TPU:4, one launch (start us, length us, event | category | flops | bytes accessed | tf_op | source)
XLA Modules:
  0.0 88.3 jit_solution(15540198276826320147)
XLA Ops:
  0.6 0.1 collective-permute-start
  0.7 2.0 %collective-permute-start.8 = (f32[3,3,48,384]{3,2,1,0:T(8,128)}, f32[3,3,48,384]{3,2,1,0:T(8,128)S(1)}, u32[]{:S(2)}, u32[]{:S(2)}) collective-permute-start(f32[3,3,48,384]{3,2,1,0:T(8,128)} %g.5), channel_id=1, source_target_pairs={{0,4},{4,0},{8,12},{12,8},{16,20},{20,16},{24,28},{28,24},{1,5},{5... | collective-permute-start | bytes 1990664 | tf_op jit(solution)/shard_map/ppermute | solution.py:570
  2.7 16.0 %collective-permute-done.pf = f32[3,3,48,384]{3,2,1,0:T(8,128)S(1)} collective-permute-done((f32[3,3,48,384]{3,2,1,0:T(8,128)}, f32[3,3,48,384]{3,2,1,0:T(8,128)S(1)}, u32[]{:S(2)}, u32[]{:S(2)}) %collective-permute-start) | collective-permute-done | bytes 663584 | tf_op jit(solution)/shard_map/ppermute | solution.py:560
  18.7 1.3 %collective-permute-start.1 = (f32[3,3,48,384]{3,2,1,0:T(8,128)S(1)}, f32[3,3,48,384]{3,2,1,0:T(8,128)S(1)}, u32[]{:S(2)}, u32[]{:S(2)}) collective-permute-start(f32[3,3,48,384]{3,2,1,0:T(8,128)S(1)} %collective-permute-done.pf), channel_id=1, source_target_pairs={{0,8},{8,16},{16,24},{12,4},{20,12},{28,20},{1,9},{9,17},{17,25},{... | collective-permute-start | bytes 1990664 | tf_op jit(solution)/shard_map/ppermute | solution.py:571
  20.0 0.8 select_reduce_fusion
  20.8 0.1 copy.9
  20.9 2.7 %collective-permute-start.6 = (f32[48,128]{1,0:T(8,128)S(1)}, f32[48,128]{1,0:T(8,128)S(1)}, u32[]{:S(2)}, u32[]{:S(2)}) collective-permute-start(f32[48,128]{1,0:T(8,128)S(1)} %pad.4.ks), channel_id=1, source_target_pairs={{0,8},{8,0},{4,12},{12,4},{16,24},{24,16},{20,28},{28,20},{1,9},{9... | collective-permute-start | bytes 73736 | tf_op jit(solution)/shard_map/ppermute | solution.py:562
  23.6 0.7 collective-permute-start.7
  24.3 0.1 stack.51.info
  24.4 0.0 copy-start
  24.4 1.1 %copy-done = f32[3,3,48,384]{3,2,1,0:T(8,128)S(1)} copy-done((f32[3,3,48,384]{3,2,1,0:T(8,128)S(1)}, f32[3,3,48,384]{3,2,1,0:T(8,128)}, u32[]{:S(2)}) %copy-start) | copy-done | bytes 663576
  25.5 0.0 copy-start.2
  25.5 1.1 %copy-done.2 = f32[3,3,48,384]{3,2,1,0:T(8,128)S(1)} copy-done((f32[3,3,48,384]{3,2,1,0:T(8,128)S(1)}, f32[3,3,48,384]{3,2,1,0:T(8,128)}, u32[]{:S(2)}) %copy-start.2) | copy-done | bytes 663576
  26.6 0.6 shard_map.59
  27.2 0.0 copy-start.1
  27.2 0.1 collective-permute-start.2
  27.3 4.5 %collective-permute-done.8.pg = f32[3,3,48,384]{3,2,1,0:T(8,128)S(1)} collective-permute-done((f32[3,3,48,384]{3,2,1,0:T(8,128)}, f32[3,3,48,384]{3,2,1,0:T(8,128)S(1)}, u32[]{:S(2)}, u32[]{:S(2)}) %collective-permute-start.8) | collective-permute-done | bytes 663584 | tf_op jit(solution)/shard_map/ppermute | solution.py:570
  31.8 0.7 collective-permute-start.3
  32.5 0.0 collective-permute-done.2.xa
  32.5 1.3 %collective-permute-start.9 = (f32[3,1,48,384]{3,2,1,0:T(8,128)S(1)}, f32[3,1,48,384]{3,2,1,0:T(8,128)S(1)}, u32[]{:S(2)}, u32[]{:S(2)}) collective-permute-start(f32[3,1,48,384]{3,2,1,0:T(8,128)S(1)} %constant_dynamic-slice_fusion.1), channel_id=1, source_target_pairs={{0,8},{8,16},{16,24},{12,4},{20,12},{28,20},{1,9},{9,17},{17,25},{... | collective-permute-start | bytes 663560 | tf_op jit(solution)/shard_map/ppermute | solution.py:574
  33.8 0.0 collective-permute-done.3.xb
  33.8 1.3 %collective-permute-start.12 = (f32[3,2,48,384]{3,2,1,0:T(8,128)S(1)}, f32[3,2,48,384]{3,2,1,0:T(8,128)S(1)}, u32[]{:S(2)}, u32[]{:S(2)}) collective-permute-start(f32[3,2,48,384]{3,2,1,0:T(8,128)S(1)} %constant_dynamic-slice_fusion), channel_id=1, source_target_pairs={{0,8},{8,16},{16,24},{12,4},{20,12},{28,20},{1,9},{9,17},{17,25},{... | collective-permute-start | bytes 1327112 | tf_op jit(solution)/shard_map/ppermute | solution.py:575
  35.1 0.6 shard_map.60
  35.8 0.0 collective-permute-done.6.ka
  35.8 5.0 %collective-permute-start.4 = (f32[96,384]{1,0:T(8,128)S(1)}, f32[96,384]{1,0:T(8,128)S(1)}, u32[]{:S(2)}, u32[]{:S(2)}) collective-permute-start(f32[96,384]{1,0:T(8,128)S(1)} %get-tuple-element.22.own), channel_id=1, source_target_pairs={{0,4},{4,0},{8,12},{12,8},{16,20},{20,16},{24,28},{28,24},{1,5},{5... | collective-permute-start | bytes 442376 | tf_op jit(solution)/shard_map/ppermute | solution.py:568
  40.7 0.0 collective-permute-done.7.kb
  40.7 2.9 %collective-permute-start.5 = (f32[96,384]{1,0:T(8,128)S(1)}, f32[96,384]{1,0:T(8,128)S(1)}, u32[]{:S(2)}, u32[]{:S(2)}) collective-permute-start(f32[96,384]{1,0:T(8,128)S(1)} %get-tuple-element.22.own), channel_id=1, source_target_pairs={{4,8},{8,4},{12,16},{16,12},{20,24},{24,20},{5,9},{9,5},{13,17},{1... | collective-permute-start | bytes 442376 | tf_op jit(solution)/shard_map/ppermute | solution.py:569
  43.7 0.2 collective-permute-done.4.partner.py
  43.9 5.3 %collective-permute-done.5.other.ry = f32[96,384]{1,0:T(8,128)S(1)} collective-permute-done((f32[96,384]{1,0:T(8,128)S(1)}, f32[96,384]{1,0:T(8,128)S(1)}, u32[]{:S(2)}, u32[]{:S(2)}) %collective-permute-start.5) | collective-permute-done | bytes 147488 | tf_op jit(solution)/shard_map/ppermute | solution.py:569
  49.2 4.5 %shard_map.61 = (f32[10,3,80,128]{3,2,1,0:T(8,128)S(1)}, f32[9,3,80,128]{3,2,1,0:T(8,128)S(1)}, f32[9,3,80,128]{3,2,1,0:T(8,128)S(1)}, f32[9,3,80,128]{3,2,1,0:T...) custom-call(s32[8]{0:T(128)S(1)} %stack.51.info, f32[48,128]{1,0:T(8,128)S(1)} %collective-permute-done.6.ka, ...), custom_call_target="tpu_custom_call" | custom-call | flops 1000000 | bytes 1000000 | tf_op jit(solution)/shard_map/pallas_call | solution.py:38
  53.8 0.0 collective-permute-done.1.rf
  53.8 0.0 copy-done.1
  53.8 0.0 copy-start.3
  53.8 5.1 %shard_map.62 = (f32[3,9,3,80,128]{4,3,2,1,0:T(8,128)S(1)}, f32[112,128]{1,0:T(8,128)S(1)}) custom-call(s32[8]{0:T(128)S(1)} %stack.51.info, f32[3,3,48,384]{3,2,1,0:T(8,128)S(1)} %copy-done.1, f32[3,3,48,384]{3,2,1,0:T(8,128)S(1)} %collective-permute-done.pf, f32[3,3,48,384]{3,2,1,0:T(8,128)S(1)} %collective-permute-done.1.rf, ...), custom_call_target="tpu_custom_call" | custom-call | flops 1000000 | bytes 1000000 | tf_op jit(solution)/shard_map/pallas_call | solution.py:38
  58.9 0.0 collective-permute-done.9.rn
  58.9 0.0 copy-done.3
  58.9 1.8 %shard_map.63 = f32[224,128]{1,0:T(8,128)S(1)} custom-call(s32[8]{0:T(128)S(1)} %stack.51.info, f32[3,3,48,384]{3,2,1,0:T(8,128)S(1)} %copy-done.3, f32[3,3,48,384]{3,2,1,0:T(8,128)S(1)} %collective-permute-done.8.pg, f32[3,1,48,384]{3,2,1,0:T(8,128)S(1)} %collective-permute-done.9.rn, f32[64,384]{1,0:T(8,128)S(1)} %get-tuple-element.20.low, ...), custom_call_target="tpu_custom_call" | custom-call | flops 1000000 | bytes 1000000 | tf_op jit(solution)/shard_map/pallas_call | solution.py:38
  60.6 7.9 %all_gather.3.rc = f32[896,128]{1,0:T(8,128)S(1)} all-gather(f32[224,128]{1,0:T(8,128)S(1)} %shard_map.63), channel_id=1, replica_groups=mesh['jet'=8,'grp'=4] {'grp'}, dimensions={0}, use_global_device_ids=true | all-gather | bytes 573440 | tf_op jit(solution)/shard_map/all_gather | solution.py:589
  68.6 2.9 %shard_map.64 = (f32[288,128]{1,0:T(8,128)S(1)}, f32[192,128]{1,0:T(8,128)S(1)}, f32[192,128]{1,0:T(8,128)S(1)}) custom-call(s32[8]{0:T(128)S(1)} %stack.51.info, f32[896,128]{1,0:T(8,128)S(1)} %all_gather.3.rc), custom_call_target="tpu_custom_call" | custom-call | flops 1000000 | bytes 1000000 | tf_op jit(solution)/shard_map/pallas_call | solution.py:38
  71.4 0.1 collective-permute-start.10
  71.5 4.9 %collective-permute-start.11 = (f32[192,128]{1,0:T(8,128)S(1)}, f32[192,128]{1,0:T(8,128)S(1)}, u32[]{:S(2)}, u32[]{:S(2)}) collective-permute-start(f32[192,128]{1,0:T(8,128)S(1)} %get-tuple-element.33), channel_id=1, source_target_pairs={{4,8},{8,4},{12,16},{16,12},{20,24},{24,20},{5,9},{9,5},{13,17},{1... | collective-permute-start | bytes 294920 | tf_op jit(solution)/shard_map/ppermute | solution.py:596
  76.4 0.1 collective-permute-done.10.ea
  76.5 2.9 %collective-permute-done.11.eb = f32[192,128]{1,0:T(8,128)S(1)} collective-permute-done((f32[192,128]{1,0:T(8,128)S(1)}, f32[192,128]{1,0:T(8,128)S(1)}, u32[]{:S(2)}, u32[]{:S(2)}) %collective-permute-start.11) | collective-permute-done | bytes 98336 | tf_op jit(solution)/shard_map/ppermute | solution.py:596
  79.4 2.6 %shard_map.65 = f32[3,3,48,384]{3,2,1,0:T(8,128)} custom-call(s32[8]{0:T(128)S(1)} %stack.51.info, f32[3,3,48,384]{3,2,1,0:T(8,128)S(1)} %copy-done.1, f32[3,9,3,80,128]{4,3,2,1,0:T(8,128)S(1)} %get-tuple-element.29.u3, f32[10,3,80,128]{3,2,1,0:T(8,128)S(1)} %get-tuple-element.23.cz, f32[9,3,80,128]{3,2,1,0:T(8,128)S(1)} %get-tuple-element.24.cx, ...), custom_call_target="tpu_custom_call" | custom-call | flops 1000000 | bytes 1000000 | tf_op jit(solution)/shard_map/pallas_call | solution.py:38
  82.0 0.0 collective-permute-done.12.rr
  82.0 6.3 %shard_map.66 = f32[3,3,48,384]{3,2,1,0:T(8,128)} custom-call(s32[8]{0:T(128)S(1)} %stack.51.info, f32[3,3,48,384]{3,2,1,0:T(8,128)S(1)} %copy-done.3, f32[3,3,48,384]{3,2,1,0:T(8,128)S(1)} %collective-permute-done.8.pg, f32[3,1,48,384]{3,2,1,0:T(8,128)S(1)} %collective-permute-done.9.rn, f32[3,2,48,384]{3,2,1,0:T(8,128)S(1)} %collective-permute-done.12.rr, ...), custom_call_target="tpu_custom_call" | custom-call | flops 1000000 | bytes 1000000 | tf_op jit(solution)/shard_map/pallas_call | solution.py:38
  (4 shorter events, 0.1 us)
Async XLA Ops:
  0.6 18.1 %collective-permute-start = (f32[3,3,48,384]{3,2,1,0:T(8,128)}, f32[3,3,48,384]{3,2,1,0:T(8,128)S(1)}, u32[]{:S(2)}, u32[]{:S(2)}) collective-permute-start(f32[3,3,48,384]{3,2,1,0:T(8,128)} %f.5), channel_id=1, source_target_pairs={{0,4},{4,0},{8,12},{12,8},{16,20},{20,16},{24,28},{28,24},{1,5},{5... | collective-permute-start | bytes 1990664 | tf_op jit(solution)/shard_map/ppermute | solution.py:560
  0.7 31.1 %collective-permute-start.8 = (f32[3,3,48,384]{3,2,1,0:T(8,128)}, f32[3,3,48,384]{3,2,1,0:T(8,128)S(1)}, u32[]{:S(2)}, u32[]{:S(2)}) collective-permute-start(f32[3,3,48,384]{3,2,1,0:T(8,128)} %g.5), channel_id=1, source_target_pairs={{0,4},{4,0},{8,12},{12,8},{16,20},{20,16},{24,28},{28,24},{1,5},{5... | collective-permute-start | bytes 1990664 | tf_op jit(solution)/shard_map/ppermute | solution.py:570
  18.7 35.1 %collective-permute-start.1 = (f32[3,3,48,384]{3,2,1,0:T(8,128)S(1)}, f32[3,3,48,384]{3,2,1,0:T(8,128)S(1)}, u32[]{:S(2)}, u32[]{:S(2)}) collective-permute-start(f32[3,3,48,384]{3,2,1,0:T(8,128)S(1)} %collective-permute-done.pf), channel_id=1, source_target_pairs={{0,8},{8,16},{16,24},{12,4},{20,12},{28,20},{1,9},{9,17},{17,25},{... | collective-permute-start | bytes 1990664 | tf_op jit(solution)/shard_map/ppermute | solution.py:571
  20.9 14.9 %collective-permute-start.6 = (f32[48,128]{1,0:T(8,128)S(1)}, f32[48,128]{1,0:T(8,128)S(1)}, u32[]{:S(2)}, u32[]{:S(2)}) collective-permute-start(f32[48,128]{1,0:T(8,128)S(1)} %pad.4.ks), channel_id=1, source_target_pairs={{0,8},{8,0},{4,12},{12,4},{16,24},{24,16},{20,28},{28,20},{1,9},{9... | collective-permute-start | bytes 73736 | tf_op jit(solution)/shard_map/ppermute | solution.py:562
  23.6 17.2 %collective-permute-start.7 = (f32[48,128]{1,0:T(8,128)S(1)}, f32[48,128]{1,0:T(8,128)S(1)}, u32[]{:S(2)}, u32[]{:S(2)}) collective-permute-start(f32[48,128]{1,0:T(8,128)S(1)} %pad.4.ks), channel_id=1, source_target_pairs={{8,16},{16,8},{12,20},{20,12},{9,17},{17,9},{13,21},{21,13},{10,18... | collective-permute-start | bytes 73736 | tf_op jit(solution)/shard_map/ppermute | solution.py:562
  24.4 1.1 %copy-start = (f32[3,3,48,384]{3,2,1,0:T(8,128)S(1)}, f32[3,3,48,384]{3,2,1,0:T(8,128)}, u32[]{:S(2)}) copy-start(f32[3,3,48,384]{3,2,1,0:T(8,128)} %f.5) | copy-start | bytes 1990660
  25.5 1.1 %copy-start.2 = (f32[3,3,48,384]{3,2,1,0:T(8,128)S(1)}, f32[3,3,48,384]{3,2,1,0:T(8,128)}, u32[]{:S(2)}) copy-start(f32[3,3,48,384]{3,2,1,0:T(8,128)} %g.5) | copy-start | bytes 1990660
  27.2 26.6 %copy-start.1 = (f32[3,3,48,384]{3,2,1,0:T(8,128)S(1)}, f32[3,3,48,384]{3,2,1,0:T(8,128)}, u32[]{:S(2)}) copy-start(f32[3,3,48,384]{3,2,1,0:T(8,128)} %f.5) | copy-start | bytes 1990660
  27.2 5.3 %collective-permute-start.2 = (f32[64,384]{1,0:T(8,128)S(1)}, f32[64,384]{1,0:T(8,128)S(1)}, u32[]{:S(2)}, u32[]{:S(2)}) collective-permute-start(f32[64,384]{1,0:T(8,128)S(1)} %get-tuple-element.18), channel_id=1, source_target_pairs={{0,1},{1,0},{2,3},{3,2},{4,5},{5,4},{6,7},{7,6},{8,9},{9,8},{10,11... | collective-permute-start | bytes 294920 | tf_op jit(solution)/shard_map/ppermute | solution.py:565
  31.8 2.1 %collective-permute-start.3 = (f32[64,384]{1,0:T(8,128)S(1)}, f32[64,384]{1,0:T(8,128)S(1)}, u32[]{:S(2)}, u32[]{:S(2)}) collective-permute-start(f32[64,384]{1,0:T(8,128)S(1)} %get-tuple-element.19), channel_id=1, source_target_pairs={{1,2},{2,1},{5,6},{6,5},{9,10},{10,9},{13,14},{14,13},{17,18},{18,... | collective-permute-start | bytes 294920 | tf_op jit(solution)/shard_map/ppermute | solution.py:565
  32.5 26.4 %collective-permute-start.9 = (f32[3,1,48,384]{3,2,1,0:T(8,128)S(1)}, f32[3,1,48,384]{3,2,1,0:T(8,128)S(1)}, u32[]{:S(2)}, u32[]{:S(2)}) collective-permute-start(f32[3,1,48,384]{3,2,1,0:T(8,128)S(1)} %constant_dynamic-slice_fusion.1), channel_id=1, source_target_pairs={{0,8},{8,16},{16,24},{12,4},{20,12},{28,20},{1,9},{9,17},{17,25},{... | collective-permute-start | bytes 663560 | tf_op jit(solution)/shard_map/ppermute | solution.py:574
  33.8 48.2 %collective-permute-start.12 = (f32[3,2,48,384]{3,2,1,0:T(8,128)S(1)}, f32[3,2,48,384]{3,2,1,0:T(8,128)S(1)}, u32[]{:S(2)}, u32[]{:S(2)}) collective-permute-start(f32[3,2,48,384]{3,2,1,0:T(8,128)S(1)} %constant_dynamic-slice_fusion), channel_id=1, source_target_pairs={{0,8},{8,16},{16,24},{12,4},{20,12},{28,20},{1,9},{9,17},{17,25},{... | collective-permute-start | bytes 1327112 | tf_op jit(solution)/shard_map/ppermute | solution.py:575
  35.8 8.1 %collective-permute-start.4 = (f32[96,384]{1,0:T(8,128)S(1)}, f32[96,384]{1,0:T(8,128)S(1)}, u32[]{:S(2)}, u32[]{:S(2)}) collective-permute-start(f32[96,384]{1,0:T(8,128)S(1)} %get-tuple-element.22.own), channel_id=1, source_target_pairs={{0,4},{4,0},{8,12},{12,8},{16,20},{20,16},{24,28},{28,24},{1,5},{5... | collective-permute-start | bytes 442376 | tf_op jit(solution)/shard_map/ppermute | solution.py:568
  40.7 8.5 %collective-permute-start.5 = (f32[96,384]{1,0:T(8,128)S(1)}, f32[96,384]{1,0:T(8,128)S(1)}, u32[]{:S(2)}, u32[]{:S(2)}) collective-permute-start(f32[96,384]{1,0:T(8,128)S(1)} %get-tuple-element.22.own), channel_id=1, source_target_pairs={{4,8},{8,4},{12,16},{16,12},{20,24},{24,20},{5,9},{9,5},{13,17},{1... | collective-permute-start | bytes 442376 | tf_op jit(solution)/shard_map/ppermute | solution.py:569
  53.8 5.1 %copy-start.3 = (f32[3,3,48,384]{3,2,1,0:T(8,128)S(1)}, f32[3,3,48,384]{3,2,1,0:T(8,128)}, u32[]{:S(2)}) copy-start(f32[3,3,48,384]{3,2,1,0:T(8,128)} %g.5) | copy-start | bytes 1990660
  71.4 5.1 %collective-permute-start.10 = (f32[192,128]{1,0:T(8,128)S(1)}, f32[192,128]{1,0:T(8,128)S(1)}, u32[]{:S(2)}, u32[]{:S(2)}) collective-permute-start(f32[192,128]{1,0:T(8,128)S(1)} %get-tuple-element.32), channel_id=1, source_target_pairs={{0,4},{4,0},{8,12},{12,8},{16,20},{20,16},{24,28},{28,24},{1,5},{5... | collective-permute-start | bytes 294920 | tf_op jit(solution)/shard_map/ppermute | solution.py:596
  71.5 7.9 %collective-permute-start.11 = (f32[192,128]{1,0:T(8,128)S(1)}, f32[192,128]{1,0:T(8,128)S(1)}, u32[]{:S(2)}, u32[]{:S(2)}) collective-permute-start(f32[192,128]{1,0:T(8,128)S(1)} %get-tuple-element.33), channel_id=1, source_target_pairs={{4,8},{8,4},{12,16},{16,12},{20,24},{24,20},{5,9},{9,5},{13,17},{1... | collective-permute-start | bytes 294920 | tf_op jit(solution)/shard_map/ppermute | solution.py:596
where the time goes:
time: 89.8 us; the launch traced here: 88.3 us
  waiting for transfers between devices  29 us (32%)
  Pallas kernels  24.3 us (27%)
  starting transfers between devices  22.9 us (26%)
  blocking collectives  7.93 us (9%)
  local copies, waits for them, and re-layouts  2.46 us (3%)
  between operations  0.9 us (1%)
    pallas_call x8, Pallas kernels, call(): pl.pallas_call(kernel, out_shape=[jax.ShapeDtypeStruct(s, F32) for s in o...  24.3 us
    ppermute x1, waiting for transfers between devices, cycle(): pf = lax.ppermute(f, 'jet', swap)  16 us
    all_gather x1, blocking collectives, cycle(): whole = lax.all_gather(rc, 'grp', axis=0, tiled=True)  7.93 us
    ppermute x1, waiting for transfers between devices, cycle(): ry = lax.ppermute(ypack, 'jet', side)  5.34 us
    ppermute x1, starting transfers between devices, cycle(): py = lax.ppermute(ypack, 'jet', swap)  4.98 us
    ppermute x2, starting transfers between devices, cycle(): ea, eb = (lax.ppermute(to_a, 'jet', swap), lax.ppermute(to_b, 'jet', side))  4.97 us
    ppermute x1, waiting for transfers between devices, cycle(): pg = lax.ppermute(g, 'jet', swap)  4.49 us
    ppermute x2, starting transfers between devices, cycle(): ka, kb = (lax.ppermute(ks, 'jet', two_a), lax.ppermute(ks, 'jet', two_b))  3.35 us
  transfers between devices with their start and end apart: 13, of which 6 were waited for; matrix products, arithmetic and copies ran while one was open for 1% of the time, Pallas kernels for 20%

commit v1 on v0

--- a/solution.py
+++ b/solution.py
@@ -32,7 +32,7 @@
     return n * (-(-shape[-2] // 8) * 8) * (-(-shape[-1] // BLOCK) * BLOCK)
 
 
-def call(kernel, outs, scratch, *args, smem=0, cost=(1000000, 1000000)):
+def call(kernel, outs, scratch, *args, smem=0, alias=None, cost=(1000000, 1000000)):
     specs = [SM] * smem + [VM] * (len(args) - smem)
     need = sum(map(padded, scratch))
     return pl.pallas_call(
@@ -41,6 +41,7 @@
         in_specs=specs,
         out_specs=[VM] * len(outs),
         scratch_shapes=[pltpu.VMEM(s, F32) for s in scratch],
+        input_output_aliases=alias or {},
         cost_estimate=pl.CostEstimate(flops=cost[0], bytes_accessed=cost[1], transcendentals=0),
         compiler_params=pltpu.CompilerParams(vmem_limit_bytes=need + (6 << 20)),
     )(*args)
@@ -50,29 +51,50 @@
     return lax.broadcasted_iota(jnp.int32, shape, dim)
 
 
-def pack_x(info, f, g, ks, to_a, to_b):
-    nf, nz, nx, ny = f.shape
+def pack_x(info, f, g, to_a, to_b):
+    nf, nz, nx, _ = f.shape
     even = info[6] == 0
-    kr = kappa_row(nf, nz)
-
-    def put(at, rows, first, last):
-        to_a[at:at + rows, 0:last.shape[1]] = jnp.where(even, last, first)
-        to_b[at:at + rows, 0:last.shape[1]] = jnp.where(even, first, last)
-
     for s, ref in enumerate((f, g)):
         for a in range(nf):
             for p in range(nz):
-                put(((s * nf + a) * nz + p) * DEEP, DEEP, ref[a, p, 0:DEEP, :], ref[a, p, nx - DEEP:nx, :])
-    for ref in (to_a, to_b):
-        ref[kr:kr + 8, :] = jnp.zeros((8, ny), F32)
-    put(kr, 4, ks[0:4, :], ks[nx - 4:nx, :])
+                at = ((s * nf + a) * nz + p) * DEEP
+                first, last = ref[a, p, 0:DEEP, :], ref[a, p, nx - DEEP:nx, :]
+                to_a[at:at + DEEP, :] = jnp.where(even, last, first)
+                to_b[at:at + DEEP, :] = jnp.where(even, first, last)
+
+
+def pack_k(info, a_in, b_in, ks, kp, ko, ka, kb, to_a, to_b, cols, *, nf, nz, nb):
+    nx = ks.shape[0]
+    n = nz * nb
+    lane = iota((nx, BLOCK), 1)
+
+    def shift(x, at):
+        return x if at % BLOCK == 0 else pltpu.roll(x, at % BLOCK, 1)
+
+    def only(x, first, count, outside=None):
+        keep = (lane >= first) & (lane < first + count)
+        if outside is not None:
+            keep = keep & (outside == 0)
+        return jnp.where(keep, x, 0.0)
+
+    up, far = info[0] == 0, info[7] == 0
+    lo1, hi1 = jnp.where(up, ko[...], kp[...]), jnp.where(up, kp[...], ko[...])
+    lo2, hi2 = jnp.where(far, kb[...], ka[...]), jnp.where(far, ka[...], kb[...])
+    kall = shift(only(lo2, n - nb, nb, info[8]), nb - n) + shift(only(lo1, 0, n, info[1]), nb) + shift(only(ks[...], 0, n), nb + n)
+    kall = kall + shift(only(hi1, 0, n, info[2]), nb + 2 * n) + shift(only(hi2, 0, nb, info[9]), nb + 3 * n)
+    cols[...] = kall
+    even = info[6] == 0
+    kr = kappa_row(nf, nz)
+    first, last = kall[0:4, :], kall[nx - 4:nx, :]
+    to_a[kr:kr + 4, 0:BLOCK] = jnp.where(even, last, first)
+    to_b[kr:kr + 4, 0:BLOCK] = jnp.where(even, first, last)
 
 
 def kappa_row(nf, nz):
     return -(-2 * nf * nz * DEEP // 8) * 8
 
 
-def pack_y(info, xa, xb, ks, out, low, high, *, nf, nz, nx):
+def pack_y(info, xa, xb, out, low, high, *, nf, nz):
     even = info[6] == 0
     low[...] = jnp.where(even, xb[...], xa[...])
     high[...] = jnp.where(even, xa[...], xb[...])
@@ -82,23 +104,6 @@
             at = (a * nz + p) * 4
             out[at:at + 2, :] = low[src + 1:src + 3, :]
             out[at + 2:at + 4, :] = high[src:src + 2, :]
-    kr = kappa_row(nf, nz)
-    at = 8 * nf * nz
-    out[at:at + nx // 2, 0:BLOCK] = ks[0:nx // 2, :]
-    out[at:at + nx // 2, BLOCK:2 * BLOCK] = ks[nx // 2:nx, :]
-    out[at:at + 4, 2 * BLOCK:3 * BLOCK] = low[kr:kr + 4, 0:BLOCK]
-    out[at + 4:at + 8, 2 * BLOCK:3 * BLOCK] = high[kr:kr + 4, 0:BLOCK]
-    out[at + 8:at + nx // 2, 2 * BLOCK:3 * BLOCK] = jnp.zeros((nx // 2 - 8, BLOCK), F32)
-
-
-def columns_of(pack, at, nx):
-    half = nx // 2
-    return (
-        (O - 4, pack[at:at + 4, 2 * BLOCK:3 * BLOCK]),
-        (O, pack[at:at + half, 0:BLOCK]),
-        (O + half, pack[at:at + half, BLOCK:2 * BLOCK]),
-        (O + nx, pack[at + 4:at + 8, 2 * BLOCK:3 * BLOCK]),
-    )
 
 
 def dot01(x, m):
@@ -243,22 +248,16 @@
         out[rows, :] = out[rows, :] + dot01(kc, pick)
 
 
-def coefficients(info, ka, kb, own, partner, other, cz, cx, cm, cp, inv, diag, kap, *, nz, nx, nb, at):
+def coefficients(info, cols, low, high, cz, cx, cm, cp, inv, diag, kap, *, nz, nx, nb, at):
     first_j, last_j, first_g, last_g = (info[i] for i in range(1, 5))
-    pbase = jnp.where(info[0] == 0, 1 + 2 * nz, 1)
-    for base, ref in ((pbase, partner), (2 + 2 * nz - pbase, other), (1 + nz, own)):
-        for row, value in columns_of(ref, at, nx):
-            n = value.shape[0]
-            for p in range(nz):
-                for b in range(nb):
-                    c = p * nb + b
-                    kap[base + p, b, row:row + n, :] = jnp.broadcast_to(value[:, c:c + 1], (n, BLOCK))
-    lo2 = jnp.where(info[7] == 0, kb[...], ka[...])
-    hi2 = jnp.where(info[7] == 0, ka[...], kb[...])
-    for b in range(nb):
-        c = (nz - 1) * nb + b
-        kap[0, b, O:O + nx, :] = jnp.broadcast_to(lo2[:, c:c + 1], (nx, BLOCK))
-        kap[3 * nz + 1, b, O:O + nx, :] = jnp.broadcast_to(hi2[:, b:b + 1], (nx, BLOCK))
+    below = jnp.where(first_g == 1, 0.0, low[at:at + 4, 0:BLOCK])
+    above = jnp.where(last_g == 1, 0.0, high[at:at + 4, 0:BLOCK])
+    for row, value in ((O - 4, below), (O, cols[...]), (O + nx, above)):
+        n = value.shape[0]
+        for p in range(3 * nz + 2):
+            for b in range(nb):
+                c = p * nb + b
+                kap[p, b, row:row + n, :] = jnp.broadcast_to(value[:, c:c + 1], (n, BLOCK))
     lane = iota((8, BLOCK), 1)
 
     def cplane(p, _):
@@ -373,31 +372,7 @@
             dst[a, q, b, pl.ds(O - 4 + j, nc + 2, stride=4), :] = part
 
 
-def fwd_after(info, f, u3, cz, cx, cm, cp, inv, est, ea, eb, filtered, ua, e):
-    nf, nz, nx, ny = f.shape
-    nb = ny // BLOCK
-    copy = lane_copy(ny)
-    coef = (cz, cx, cm, cp, inv)
-    qa = jnp.where(info[0] == 0, 2 * nz, nz - 1)
-    for ref, slots, base in ((est, nz, nz), (ea, 1, qa), (eb, 1, 3 * nz - 1 - qa)):
-        n = nf * slots * 16
-        e[0:n, :] = dot01(ref[0:n, :], copy)
-        for a in range(nf):
-            for i in range(slots):
-                prolong(ua, e, a * slots + i, a, base + i, nx, nb)
-
-    def one(p, _):
-        for a in range(nf):
-            for b in range(nb):
-                for r in rows_of(True, nx):
-                    ua[a, p, b, r:r + 8, :] = ua[a, p, b, r:r + 8, :] + u3[a, p, b, r:r + 8, :]
-        return 0
-
-    lax.fori_loop(nz - 1, 2 * nz + 1, one, 0)
-    final(filtered, ua, f, coef, nz, nx)
-
-
-def adj_after(info, g, pg, rn, rr, low, high, py, ry, cz, cx, cm, cp, inv, est, ea, eb, adjoint, gx, ua, ub, e):
+def middle(info, u3, g, pg, rn, rr, low, high, py, ry, inv, est, uf, gx, ug, tmp, e):
     nf, nz, nx, ny = g.shape
     nb = ny // BLOCK
     par = info[0]
@@ -418,26 +393,57 @@
                 c = slice(b * BLOCK, (b + 1) * BLOCK)
                 gx[a, rbase + p, b, O - width:O, :] = ry[lo_row:lo_row + width, c]
                 gx[a, rbase + p, b, O + nx:O + nx + width, :] = ry[hi_row:hi_row + width, c]
-    copy = lane_copy(ny)
-    coef = (cz, cx, cm, cp, inv)
-    n = nf * nz * 16
-    for ref, at, base in ((est, n, nz), (ea, nf * 16, pbase), (eb, nf * 16, rbase)):
-        e[...] = dot01(ref[at:at + n, :], copy)
+
+    def one(p, _):
+        start(ug, gx, inv, p, nx, nb, nf)
+        return 0
+
+    lax.fori_loop(0, 3 * nz, one, 0)
+    e[...] = dot01(est[...], lane_copy(ny))
+    for s, dst in enumerate((uf, ug)):
         for a in range(nf):
             for i in range(nz):
-                prolong(ua, e, a * nz + i, a, base + i, nx, nb)
-
-    def one(p, _):
-        for b in range(nb):
-            for r in rows_of(True, nx):
-                w = inv[p, b, r:r + 8, :]
-                for a in range(nf):
-                    ua[a, p, b, r:r + 8, :] = ua[a, p, b, r:r + 8, :] + w * gx[a, p, b, r:r + 8, :]
-        return 0
-
-    lax.fori_loop(0, 3 * nz, one, 0)
-    three(ua, ub, gx, coef, nz, nx)
-    final(adjoint, ua, g, coef, nz, nx)
+                prolong(tmp, e, (s * nf + a) * nz + i, a, i, nx, nb)
+
+        def add(i, _):
+            for a in range(nf):
+                for b in range(nb):
+                    for r in rows_of(True, nx):
+                        dst[a, nz + i, b, r:r + 8, :] = dst[a, nz + i, b, r:r + 8, :] + tmp[a, i, b, r:r + 8, :]
+            return 0
+
+        lax.fori_loop(0, nz, add, 0)
+
+
+def last(info, f, g, gx, uf_in, ug_in, cz, cx, cm, cp, inv, ea, eb, filtered, adjoint, uf, ug, ub, e):
+    nf, nz, nx, ny = f.shape
+    nb = ny // BLOCK
+    coef = (cz, cx, cm, cp, inv)
+    pbase = jnp.where(info[0] == 0, 2 * nz, 0)
+    copy = lane_copy(ny)
+    edge = jnp.where(info[0] == 0, 2 * nz, nz - 1)
+    for ref, base, q in ((ea, pbase, edge), (eb, 2 * nz - pbase, 3 * nz - 1 - edge)):
+        e[...] = dot01(ref[...], copy)
+        for a in range(nf):
+            prolong(ub, e, a, a, 0, nx, nb)
+            for i in range(nz):
+                prolong(ub, e, nf + a * nz + i, a, 1 + i, nx, nb)
+        for a in range(nf):
+            for b in range(nb):
+                for r in rows_of(True, nx):
+                    uf[a, q, b, r:r + 8, :] = uf[a, q, b, r:r + 8, :] + ub[a, 0, b, r:r + 8, :]
+
+        def add(i, _):
+            for a in range(nf):
+                for b in range(nb):
+                    for r in rows_of(True, nx):
+                        ug[a, base + i, b, r:r + 8, :] = ug[a, base + i, b, r:r + 8, :] + ub[a, 1 + i, b, r:r + 8, :]
+            return 0
+
+        lax.fori_loop(0, nz, add, 0)
+    final(filtered, uf, f, coef, nz, nx)
+    three(ug, ub, gx, coef, nz, nx)
+    final(adjoint, ug, g, coef, nz, nx)
 
 
 def coarse(info, rc, est, to_a, to_b, full, e0, e1, ck, cf, *, nf, nz, ng, nc, nb):
@@ -540,47 +546,53 @@
     nb = ny // BLOCK
     nc = nx // 4
     nj, ng = lax.axis_size("jet"), lax.axis_size("grp")
-    assert nz == DEEP and nj % 2 == 0
+    assert nz == DEEP and nj % 4 == 0 and ng % 2 == 0
     j, gi = lax.axis_index("jet"), lax.axis_index("grp")
     par = j % 2
     zp = (j // 2) % 2
-    info = jnp.stack([par, (j == 0) * 1, (j == nj - 1) * 1, (gi == 0) * 1, (gi == ng - 1) * 1, gi, gi % 2, zp]).astype(jnp.int32)
+    info = jnp.stack([par, (j == 0) * 1, (j == nj - 1) * 1, (gi == 0) * 1, (gi == ng - 1) * 1, gi, gi % 2, zp, (j < 2) * 1, (j >= nj - 2) * 1]).astype(jnp.int32)
 
     def both(pairs):
         return [p for a, b in pairs for p in ((a, b), (b, a))]
 
     swap = both([(i, i + 1) for i in range(0, nj, 2)])
-    side = both([(i, i + 1) for i in range(1, nj - 1, 2)])
-    relay = [(i, i + 2) for i in range(0, nj - 2, 2)] + [(i, i - 2) for i in range(3, nj, 2)]
-    two_a = both([(i, i + 2) for i in range(nj - 2) if (i // 2) % 2 == 0])
-    two_b = both([(i, i + 2) for i in range(nj - 2) if (i // 2) % 2 == 1])
-    x_a = both([(i, i + 1) for i in range(0, ng - 1, 2)])
-    x_b = both([(i, i + 1) for i in range(1, ng - 1, 2)])
-
-    pf = lax.ppermute(f, "jet", swap)
+    side = both([(i, (i + 1) % nj) for i in range(1, nj, 2)])
+    inner = [pair for pair in side if abs(pair[0] - pair[1]) == 1]
+    relay = [(i, (i + 2) % nj if i % 2 == 0 else (i - 2) % nj) for i in range(nj)]
+    two_a = both([(i, (i + 2) % nj) for i in range(nj) if (i // 2) % 2 == 0])
+    two_b = both([(i, (i + 2) % nj) for i in range(nj) if (i // 2) % 2 == 1])
+    x_a = both([(i, i + 1) for i in range(0, ng, 2)])
+    x_b = both([(i, (i + 1) % ng) for i in range(1, ng, 2)])
+
+    def send(x, axis, perm):
+        return lax.ppermute(x, axis, perm)
+
+    pf = send(f, "jet", swap)
     ks = kappa_columns(width_class)
-    ka, kb = lax.ppermute(ks, "jet", two_a), lax.ppermute(ks, "jet", two_b)
+    near_k = [send(ks, "jet", swap), send(ks, "jet", side), send(ks, "jet", two_a), send(ks, "jet", two_b)]
     xs = (kappa_row(nf, nz) + 8, ny)
-    to_a, to_b = call(pack_x, [xs] * 2, [], info, f, g, ks, smem=1)
-    xa, xb = lax.ppermute(to_a, "grp", x_a), lax.ppermute(to_b, "grp", x_b)
-    krow = 8 * nf * nz
-    ypack, low, high = call(functools.partial(pack_y, nf=nf, nz=nz, nx=nx), [(krow + nx // 2, ny), xs, xs], [], info, xa, xb, ks, smem=1)
-    py = lax.ppermute(ypack, "jet", swap)
-    ry = lax.ppermute(ypack, "jet", side)
-    pg = lax.ppermute(g, "jet", swap)
-    rf = lax.ppermute(pf, "jet", relay)
+    to_a, to_b = call(pack_x, [xs, xs], [], info, f, g, smem=1)
+    to_a, to_b, cols = call(
+        functools.partial(pack_k, nf=nf, nz=nz, nb=nb), [xs, xs, (nx, BLOCK)], [],
+        info, to_a, to_b, ks, *near_k, smem=1, alias={1: 0, 2: 1})
+    xa, xb = send(to_a, "grp", x_a), send(to_b, "grp", x_b)
+    ypack, low, high = call(functools.partial(pack_y, nf=nf, nz=nz), [(8 * nf * nz, ny), xs, xs], [], info, xa, xb, smem=1)
+    py = send(ypack, "jet", swap)
+    ry = send(ypack, "jet", side)
+    pg = send(g, "jet", swap)
+    rf = send(pf, "jet", relay)
     near = lax.dynamic_slice_in_dim(pg, (1 - par) * (nz - 1), 1, 1)
     rest = lax.dynamic_slice_in_dim(pg, par, nz - 1, 1)
-    rn = lax.ppermute(near, "jet", relay)
-    rr = lax.ppermute(rest, "jet", relay)
+    rn = send(near, "jet", relay)
+    rr = send(rest, "jet", relay)
 
     xr = nx + 32
     deep = (nf, 3 * nz, nb, xr, BLOCK)
     co = (3 * nz, nb, xr, BLOCK)
     coefs = call(
-        functools.partial(coefficients, nz=nz, nx=nx, nb=nb, at=krow),
+        functools.partial(coefficients, nz=nz, nx=nx, nb=nb, at=kappa_row(nf, nz)),
         [(3 * nz + 1, nb, xr, BLOCK), co, co, co, co, (nz, nb, xr, BLOCK)], [(3 * nz + 2, nb, xr, BLOCK)],
-        info, ka, kb, ypack, py, ry, smem=1)
+        info, cols, low, high, smem=1)
     coef, diag = coefs[:5], coefs[5]
     rows = -(-nf * nz * nc // 8) * 8
     scratch = [(nb, nf * nz, nx, BLOCK), (rows, BLOCK)]
@@ -593,9 +605,13 @@
     est, to_a, to_b = call(
         functools.partial(coarse, nf=nf, nz=nz, ng=ng, nc=nc, nb=nb),
         [(2 * nf * nz * 16, BLOCK), sent, sent], solve, info, whole, smem=1)
-    ea, eb = lax.ppermute(to_a, "jet", swap), lax.ppermute(to_b, "jet", side)
-    (filtered,) = call(fwd_after, [f.shape], [deep, (nf * nz * 16, ny)], info, f, u3, *coef, est, ea, eb, smem=1)
-    (adjoint,) = call(adj_after, [g.shape], [deep, deep, deep, (nf * nz * 16, ny)], info, g, pg, rn, rr, low, high, py, ry, *coef, est, ea, eb, smem=1)
+    ea, eb = send(to_a, "jet", swap), send(to_b, "jet", inner)
+    uf, gx, ug = call(
+        middle, [deep] * 3, [deep, (2 * nf * nz * 16, ny)],
+        info, u3, g, pg, rn, rr, low, high, py, ry, coef[4], est, smem=1, alias={1: 0})
+    filtered, adjoint, _, _ = call(
+        last, [f.shape, g.shape, deep, deep], [deep, (nf * (nz + 1) * 16, ny)],
+        info, f, g, gx, uf, ug, *coef, ea, eb, smem=1, alias={4: 2, 5: 3})
     return filtered, adjoint
 
 

time: 89.8 us -> 96.5 us (1.075)
  waiting for transfers between devices: 29 us -> 38.8 us
  blocking collectives: 7.93 us -> 6.6 us
  starting transfers between devices: 22.9 us -> 21.7 us
    ppermute x13 -> x15, waiting for transfers between devices: 29 us -> 38.8 us  [send(): return lax.ppermute(x, axis, perm)]
    all_gather x1, blocking collectives: 7.93 us -> 6.6 us  [cycle(): whole = lax.all_gather(rc, 'grp', axis=0, tiled=True)]
    ppermute x13 -> x15, starting transfers between devices: 22.9 us -> 21.7 us  [send(): return lax.ppermute(x, axis, perm)]
    pallas_call x8 -> x9, Pallas kernels: 24.3 us -> 24.8 us  [call(): pl.pallas_call(kernel, out_shape=[jax.ShapeDtypeStruct(s, F32) for s in o...]
  transfers between devices with their start and end apart: 13 -> 15, of which waited for: 6 -> 5; matrix products, arithmetic and copies ran while one was open for 1% -> 1% of each run, Pallas kernels for 20% -> 18%
where the time goes in v1:
time: 96.5 us; the launch traced here: 96 us
  waiting for transfers between devices  38.8 us (40%)
  Pallas kernels  24.8 us (26%)
  starting transfers between devices  21.7 us (22%)
  blocking collectives  6.6 us (7%)
  local copies, waits for them, and re-layouts  2.43 us (3%)
    ppermute x15, waiting for transfers between devices, send(): return lax.ppermute(x, axis, perm)  38.8 us
    pallas_call x9, Pallas kernels, call(): pl.pallas_call(kernel, out_shape=[jax.ShapeDtypeStruct(s, F32) for s in o...  24.8 us
    ppermute x15, starting transfers between devices, send(): return lax.ppermute(x, axis, perm)  21.7 us
    all_gather x1, blocking collectives, cycle(): whole = lax.all_gather(rc, 'grp', axis=0, tiled=True)  6.6 us
    unnamed x8, local copies, waits for them, and re-layouts  2.19 us
  transfers between devices with their start and end apart: 15, of which 5 were waited for; matrix products, arithmetic and copies ran while one was open for 1% of the time, Pallas kernels for 18%

profile of v1, /device:TPU:4, one launch (start us, length us, event | category | flops | bytes accessed | tf_op | source)
XLA Modules:
  0.0 96.0 jit_solution(5142298556603793953)
XLA Ops:
  0.6 0.1 collective-permute-start
  0.7 2.0 %collective-permute-start.10 = (f32[3,3,48,384]{3,2,1,0:T(8,128)}, f32[3,3,48,384]{3,2,1,0:T(8,128)S(1)}, u32[]{:S(2)}, u32[]{:S(2)}) collective-permute-start(f32[3,3,48,384]{3,2,1,0:T(8,128)} %g.7), channel_id=1, source_target_pairs={{0,4},{4,0},{8,12},{12,8},{16,20},{20,16},{24,28},{28,24},{1,5},{5... | collective-permute-start | bytes 1990664 | tf_op jit(solution)/shard_map/ppermute | solution.py:568
  2.7 16.0 %collective-permute-done.pf = f32[3,3,48,384]{3,2,1,0:T(8,128)S(1)} collective-permute-done((f32[3,3,48,384]{3,2,1,0:T(8,128)}, f32[3,3,48,384]{3,2,1,0:T(8,128)S(1)}, u32[]{:S(2)}, u32[]{:S(2)}) %collective-permute-start) | collective-permute-done | bytes 663584 | tf_op jit(solution)/shard_map/ppermute | solution.py:568
  18.7 3.6 %collective-permute-start.1 = (f32[3,3,48,384]{3,2,1,0:T(8,128)S(1)}, f32[3,3,48,384]{3,2,1,0:T(8,128)S(1)}, u32[]{:S(2)}, u32[]{:S(2)}) collective-permute-start(f32[3,3,48,384]{3,2,1,0:T(8,128)S(1)} %collective-permute-done.pf), channel_id=1, source_target_pairs={{0,8},{4,28},{8,16},{12,4},{16,24},{20,12},{24,0},{28,20},{1,9},{5... | collective-permute-start | bytes 1990664 | tf_op jit(solution)/shard_map/ppermute | solution.py:568
  22.3 0.8 select_reduce_fusion
  23.1 0.1 copy.14
  23.2 0.5 collective-permute-start.5
  23.7 0.0 collective-permute-start.4
  23.7 1.5 %collective-permute-start.3 = (f32[48,128]{1,0:T(8,128)S(1)}, f32[48,128]{1,0:T(8,128)S(1)}, u32[]{:S(2)}, u32[]{:S(2)}) collective-permute-start(f32[48,128]{1,0:T(8,128)S(1)} %pad.4.ks), channel_id=1, source_target_pairs={{4,8},{8,4},{12,16},{16,12},{20,24},{24,20},{28,0},{0,28},{5,9},{9... | collective-permute-start | bytes 73736 | tf_op jit(solution)/shard_map/ppermute | solution.py:568
  25.2 11.2 %collective-permute-done.5.kb = f32[48,128]{1,0:T(8,128)S(1)} collective-permute-done((f32[48,128]{1,0:T(8,128)S(1)}, f32[48,128]{1,0:T(8,128)S(1)}, u32[]{:S(2)}, u32[]{:S(2)}) %collective-permute-start.5) | collective-permute-done | bytes 24608 | tf_op jit(solution)/shard_map/ppermute | solution.py:568
  36.4 0.4 collective-permute-start.2
  36.9 0.1 stack.67.info
  36.9 0.0 copy-start
  36.9 1.1 %copy-done = f32[3,3,48,384]{3,2,1,0:T(8,128)S(1)} copy-done((f32[3,3,48,384]{3,2,1,0:T(8,128)S(1)}, f32[3,3,48,384]{3,2,1,0:T(8,128)}, u32[]{:S(2)}) %copy-start) | copy-done | bytes 663576
  38.0 0.0 copy-start.2
  38.0 1.1 %copy-done.2 = f32[3,3,48,384]{3,2,1,0:T(8,128)S(1)} copy-done((f32[3,3,48,384]{3,2,1,0:T(8,128)S(1)}, f32[3,3,48,384]{3,2,1,0:T(8,128)}, u32[]{:S(2)}) %copy-start.2) | copy-done | bytes 663576
  39.1 0.0 copy-start.3
  39.1 0.6 shard_map.59
  39.7 0.0 collective-permute-done.4.ka
  39.7 0.0 collective-permute-done.3.ko
  39.8 0.5 collective-permute-done.2.kp
  40.3 0.6 shard_map.60
  40.9 0.1 collective-permute-start.6
  41.0 1.6 %collective-permute-start.7 = (f32[64,384]{1,0:T(8,128)S(1)}, f32[64,384]{1,0:T(8,128)S(1)}, u32[]{:S(2)}, u32[]{:S(2)}) collective-permute-start(f32[64,384]{1,0:T(8,128)S(1)} %get-tuple-element.29), channel_id=1, source_target_pairs={{1,2},{2,1},{3,0},{0,3},{5,6},{6,5},{7,4},{4,7},{9,10},{10,9},{11,... | collective-permute-start | bytes 294920 | tf_op jit(solution)/shard_map/ppermute | solution.py:568
  42.6 0.0 collective-permute-done.10.pg
  42.6 3.5 %collective-permute-start.11 = (f32[3,1,48,384]{3,2,1,0:T(8,128)S(1)}, f32[3,1,48,384]{3,2,1,0:T(8,128)S(1)}, u32[]{:S(2)}, u32[]{:S(2)}) collective-permute-start(f32[3,1,48,384]{3,2,1,0:T(8,128)S(1)} %constant_dynamic-slice_fusion.1), channel_id=1, source_target_pairs={{0,8},{4,28},{8,16},{12,4},{16,24},{20,12},{24,0},{28,20},{1,9},{5... | collective-permute-start | bytes 663560 | tf_op jit(solution)/shard_map/ppermute | solution.py:568
  46.1 0.1 collective-permute-start.12
  46.2 0.0 collective-permute-done.6.xa
  46.2 0.0 collective-permute-done.7.xb
  46.2 0.6 shard_map.61
  46.8 1.7 %collective-permute-start.9 = (f32[72,384]{1,0:T(8,128)S(1)}, f32[72,384]{1,0:T(8,128)S(1)}, u32[]{:S(2)}, u32[]{:S(2)}) collective-permute-start(f32[72,384]{1,0:T(8,128)S(1)} %get-tuple-element.32), channel_id=1, source_target_pairs={{4,8},{8,4},{12,16},{16,12},{20,24},{24,20},{28,0},{0,28},{5,9},{9... | collective-permute-start | bytes 331784 | tf_op jit(solution)/shard_map/ppermute | solution.py:568
  48.5 2.6 %collective-permute-start.8 = (f32[72,384]{1,0:T(8,128)S(1)}, f32[72,384]{1,0:T(8,128)S(1)}, u32[]{:S(2)}, u32[]{:S(2)}) collective-permute-start(f32[72,384]{1,0:T(8,128)S(1)} %get-tuple-element.32), channel_id=1, source_target_pairs={{0,4},{4,0},{8,12},{12,8},{16,20},{20,16},{24,28},{28,24},{1,5},{5... | collective-permute-start | bytes 331784 | tf_op jit(solution)/shard_map/ppermute | solution.py:568
  51.1 4.5 %shard_map.62 = (f32[10,3,80,128]{3,2,1,0:T(8,128)S(1)}, f32[9,3,80,128]{3,2,1,0:T(8,128)S(1)}, f32[9,3,80,128]{3,2,1,0:T(8,128)S(1)}, f32[9,3,80,128]{3,2,1,0:T...) custom-call(s32[10]{0:T(128)S(1)} %stack.67.info, f32[48,128]{1,0:T(8,128)S(1)} %get-tuple-element.33.cols, ...), custom_call_target="tpu_custom_call" | custom-call | flops 1000000 | bytes 1000000 | tf_op jit(solution)/shard_map/pallas_call | solution.py:38
  55.6 8.6 %collective-permute-done.9.ry = f32[72,384]{1,0:T(8,128)S(1)} collective-permute-done((f32[72,384]{1,0:T(8,128)S(1)}, f32[72,384]{1,0:T(8,128)S(1)}, u32[]{:S(2)}, u32[]{:S(2)}) %collective-permute-start.9) | collective-permute-done | bytes 110624 | tf_op jit(solution)/shard_map/ppermute | solution.py:568
  64.3 0.0 collective-permute-done.8.py
  64.3 0.0 collective-permute-done.1.rf
  64.3 0.0 copy-done.3
  64.3 0.0 copy-start.1
  64.3 5.2 %shard_map.63 = (f32[3,9,3,80,128]{4,3,2,1,0:T(8,128)S(1)}, f32[112,128]{1,0:T(8,128)S(1)}) custom-call(s32[10]{0:T(128)S(1)} %stack.67.info, f32[3,3,48,384]{3,2,1,0:T(8,128)S(1)} %copy-done.3, f32[3,3,48,384]{3,2,1,0:T(8,128)S(1)} %collective-permute-done.pf, f32[3,3,48,384]{3,2,1,0:T(8,128)S(1)} %collective-permute-done.1.rf, ...), custom_call_target="tpu_custom_call" | custom-call | flops 1000000 | bytes 1000000 | tf_op jit(solution)/shard_map/pallas_call | solution.py:38
  69.5 0.0 collective-permute-done.11.rn
  69.5 0.0 copy-done.1
  69.5 1.7 %shard_map.64 = f32[224,128]{1,0:T(8,128)S(1)} custom-call(s32[10]{0:T(128)S(1)} %stack.67.info, f32[3,3,48,384]{3,2,1,0:T(8,128)S(1)} %copy-done.1, f32[3,3,48,384]{3,2,1,0:T(8,128)S(1)} %collective-permute-done.10.pg, f32[3,1,48,384]{3,2,1,0:T(8,128)S(1)} %collective-permute-done.11.rn, f32[64,384]{1,0:T(8,128)S(1)} %get-tuple-element.30.low, ...), custom_call_target="tpu_custom_call" | custom-call | flops 1000000 | bytes 1000000 | tf_op jit(solution)/shard_map/pallas_call | solution.py:38
  71.2 6.6 %all_gather.3.rc = f32[896,128]{1,0:T(8,128)S(1)} all-gather(f32[224,128]{1,0:T(8,128)S(1)} %shard_map.64), channel_id=1, replica_groups=mesh['jet'=8,'grp'=4] {'grp'}, dimensions={0}, use_global_device_ids=true | all-gather | bytes 573440 | tf_op jit(solution)/shard_map/all_gather | solution.py:601
  77.8 2.9 %shard_map.65 = (f32[288,128]{1,0:T(8,128)S(1)}, f32[192,128]{1,0:T(8,128)S(1)}, f32[192,128]{1,0:T(8,128)S(1)}) custom-call(s32[10]{0:T(128)S(1)} %stack.67.info, f32[896,128]{1,0:T(8,128)S(1)} %all_gather.3.rc), custom_call_target="tpu_custom_call" | custom-call | flops 1000000 | bytes 1000000 | tf_op jit(solution)/shard_map/pallas_call | solution.py:38
  80.7 0.6 collective-permute-start.13
  81.3 3.4 %collective-permute-start.14 = (f32[192,128]{1,0:T(8,128)S(1)}, f32[192,128]{1,0:T(8,128)S(1)}, u32[]{:S(2)}, u32[]{:S(2)}) collective-permute-start(f32[192,128]{1,0:T(8,128)S(1)} %get-tuple-element.47), channel_id=1, source_target_pairs={{4,8},{8,4},{12,16},{16,12},{20,24},{24,20},{5,9},{9,5},{13,17},{1... | collective-permute-start | bytes 294920 | tf_op jit(solution)/shard_map/ppermute | solution.py:568
  84.7 0.0 collective-permute-done.12.rr
  84.7 1.6 %shard_map.66 = (f32[3,9,3,80,128]{4,3,2,1,0:T(8,128)S(1)}, f32[3,9,3,80,128]{4,3,2,1,0:T(8,128)S(1)}, f32[3,9,3,80,128]{4,3,2,1,0:T(8,128)S(1)}) custom-call(s32[10]{0:T(128)S(1)} %stack.67.info, f32[3,9,3,80,128]{4,3,2,1,0:T(8,128)S(1)} %get-tuple-element.40.u3, f32[3,3,48,384]{3,2,1,0:T(8,128)S(1)} %copy-done.1, ...), custom_call_target="tpu_custom_call", output_to_operand_aliasing={{0}: (1, {})} | custom-call | flops 1000000 | bytes 1000000 | tf_op jit(solution)/shard_map/pallas_call | solution.py:38
  86.3 0.0 collective-permute-done.13.ea
  86.3 2.5 %collective-permute-done.14.eb = f32[192,128]{1,0:T(8,128)S(1)} collective-permute-done((f32[192,128]{1,0:T(8,128)S(1)}, f32[192,128]{1,0:T(8,128)S(1)}, u32[]{:S(2)}, u32[]{:S(2)}) %collective-permute-start.14) | collective-permute-done | bytes 98336 | tf_op jit(solution)/shard_map/ppermute | solution.py:568
  88.8 7.1 %shard_map.67 = (f32[3,3,48,384]{3,2,1,0:T(8,128)}, f32[3,3,48,384]{3,2,1,0:T(8,128)}, f32[3,9,3,80,128]{4,3,2,1,0:T(8,128)S(1)}, f32[3,9,3,80,128]{4,3,2,1,0:T(8,128)S(1)}) custom-call(s32[10]{0:T(128)S(1)} %stack.67.info, f32[3,3,48,384]{3,2,1,0:T(8,128)S(1)} %copy-done.3, ...), custom_call_target="tpu_custom_call", output_to_operand_aliasing={{2}: (4, {}), {3}: (5, {})} | custom-call | flops 1000000 | bytes 1000000 | tf_op jit(solution)/shard_map/pallas_call | solution.py:38
  (4 shorter events, 0.1 us)
Async XLA Ops:
  0.6 18.1 %collective-permute-start = (f32[3,3,48,384]{3,2,1,0:T(8,128)}, f32[3,3,48,384]{3,2,1,0:T(8,128)S(1)}, u32[]{:S(2)}, u32[]{:S(2)}) collective-permute-start(f32[3,3,48,384]{3,2,1,0:T(8,128)} %f.5), channel_id=1, source_target_pairs={{0,4},{4,0},{8,12},{12,8},{16,20},{20,16},{24,28},{28,24},{1,5},{5... | collective-permute-start | bytes 1990664 | tf_op jit(solution)/shard_map/ppermute | solution.py:568
  0.7 41.9 %collective-permute-start.10 = (f32[3,3,48,384]{3,2,1,0:T(8,128)}, f32[3,3,48,384]{3,2,1,0:T(8,128)S(1)}, u32[]{:S(2)}, u32[]{:S(2)}) collective-permute-start(f32[3,3,48,384]{3,2,1,0:T(8,128)} %g.7), channel_id=1, source_target_pairs={{0,4},{4,0},{8,12},{12,8},{16,20},{20,16},{24,28},{28,24},{1,5},{5... | collective-permute-start | bytes 1990664 | tf_op jit(solution)/shard_map/ppermute | solution.py:568
  18.7 45.6 %collective-permute-start.1 = (f32[3,3,48,384]{3,2,1,0:T(8,128)S(1)}, f32[3,3,48,384]{3,2,1,0:T(8,128)S(1)}, u32[]{:S(2)}, u32[]{:S(2)}) collective-permute-start(f32[3,3,48,384]{3,2,1,0:T(8,128)S(1)} %collective-permute-done.pf), channel_id=1, source_target_pairs={{0,8},{4,28},{8,16},{12,4},{16,24},{20,12},{24,0},{28,20},{1,9},{5... | collective-permute-start | bytes 1990664 | tf_op jit(solution)/shard_map/ppermute | solution.py:568
  23.2 13.2 %collective-permute-start.5 = (f32[48,128]{1,0:T(8,128)S(1)}, f32[48,128]{1,0:T(8,128)S(1)}, u32[]{:S(2)}, u32[]{:S(2)}) collective-permute-start(f32[48,128]{1,0:T(8,128)S(1)} %pad.4.ks), channel_id=1, source_target_pairs={{8,16},{16,8},{12,20},{20,12},{24,0},{0,24},{28,4},{4,28},{9,17},{... | collective-permute-start | bytes 73736 | tf_op jit(solution)/shard_map/ppermute | solution.py:568
  23.7 16.0 %collective-permute-start.4 = (f32[48,128]{1,0:T(8,128)S(1)}, f32[48,128]{1,0:T(8,128)S(1)}, u32[]{:S(2)}, u32[]{:S(2)}) collective-permute-start(f32[48,128]{1,0:T(8,128)S(1)} %pad.4.ks), channel_id=1, source_target_pairs={{0,8},{8,0},{4,12},{12,4},{16,24},{24,16},{20,28},{28,20},{1,9},{9... | collective-permute-start | bytes 73736 | tf_op jit(solution)/shard_map/ppermute | solution.py:568
  23.7 16.0 %collective-permute-start.3 = (f32[48,128]{1,0:T(8,128)S(1)}, f32[48,128]{1,0:T(8,128)S(1)}, u32[]{:S(2)}, u32[]{:S(2)}) collective-permute-start(f32[48,128]{1,0:T(8,128)S(1)} %pad.4.ks), channel_id=1, source_target_pairs={{4,8},{8,4},{12,16},{16,12},{20,24},{24,20},{28,0},{0,28},{5,9},{9... | collective-permute-start | bytes 73736 | tf_op jit(solution)/shard_map/ppermute | solution.py:568
  36.4 3.8 %collective-permute-start.2 = (f32[48,128]{1,0:T(8,128)S(1)}, f32[48,128]{1,0:T(8,128)S(1)}, u32[]{:S(2)}, u32[]{:S(2)}) collective-permute-start(f32[48,128]{1,0:T(8,128)S(1)} %pad.4.ks), channel_id=1, source_target_pairs={{0,4},{4,0},{8,12},{12,8},{16,20},{20,16},{24,28},{28,24},{1,5},{5... | collective-permute-start | bytes 73736 | tf_op jit(solution)/shard_map/ppermute | solution.py:568
  36.9 1.1 %copy-start = (f32[3,3,48,384]{3,2,1,0:T(8,128)S(1)}, f32[3,3,48,384]{3,2,1,0:T(8,128)}, u32[]{:S(2)}) copy-start(f32[3,3,48,384]{3,2,1,0:T(8,128)} %g.7) | copy-start | bytes 1990660
  38.0 1.1 %copy-start.2 = (f32[3,3,48,384]{3,2,1,0:T(8,128)S(1)}, f32[3,3,48,384]{3,2,1,0:T(8,128)}, u32[]{:S(2)}) copy-start(f32[3,3,48,384]{3,2,1,0:T(8,128)} %f.5) | copy-start | bytes 1990660
  39.1 25.1 %copy-start.3 = (f32[3,3,48,384]{3,2,1,0:T(8,128)S(1)}, f32[3,3,48,384]{3,2,1,0:T(8,128)}, u32[]{:S(2)}) copy-start(f32[3,3,48,384]{3,2,1,0:T(8,128)} %f.5) | copy-start | bytes 1990660
  40.9 5.3 %collective-permute-start.6 = (f32[64,384]{1,0:T(8,128)S(1)}, f32[64,384]{1,0:T(8,128)S(1)}, u32[]{:S(2)}, u32[]{:S(2)}) collective-permute-start(f32[64,384]{1,0:T(8,128)S(1)} %get-tuple-element.28), channel_id=1, source_target_pairs={{0,1},{1,0},{2,3},{3,2},{4,5},{5,4},{6,7},{7,6},{8,9},{9,8},{10,11... | collective-permute-start | bytes 294920 | tf_op jit(solution)/shard_map/ppermute | solution.py:568
  41.0 5.2 %collective-permute-start.7 = (f32[64,384]{1,0:T(8,128)S(1)}, f32[64,384]{1,0:T(8,128)S(1)}, u32[]{:S(2)}, u32[]{:S(2)}) collective-permute-start(f32[64,384]{1,0:T(8,128)S(1)} %get-tuple-element.29), channel_id=1, source_target_pairs={{1,2},{2,1},{3,0},{0,3},{5,6},{6,5},{7,4},{4,7},{9,10},{10,9},{11,... | collective-permute-start | bytes 294920 | tf_op jit(solution)/shard_map/ppermute | solution.py:568
  42.6 26.9 %collective-permute-start.11 = (f32[3,1,48,384]{3,2,1,0:T(8,128)S(1)}, f32[3,1,48,384]{3,2,1,0:T(8,128)S(1)}, u32[]{:S(2)}, u32[]{:S(2)}) collective-permute-start(f32[3,1,48,384]{3,2,1,0:T(8,128)S(1)} %constant_dynamic-slice_fusion.1), channel_id=1, source_target_pairs={{0,8},{4,28},{8,16},{12,4},{16,24},{20,12},{24,0},{28,20},{1,9},{5... | collective-permute-start | bytes 663560 | tf_op jit(solution)/shard_map/ppermute | solution.py:568
  46.1 38.5 %collective-permute-start.12 = (f32[3,2,48,384]{3,2,1,0:T(8,128)S(1)}, f32[3,2,48,384]{3,2,1,0:T(8,128)S(1)}, u32[]{:S(2)}, u32[]{:S(2)}) collective-permute-start(f32[3,2,48,384]{3,2,1,0:T(8,128)S(1)} %constant_dynamic-slice_fusion), channel_id=1, source_target_pairs={{0,8},{4,28},{8,16},{12,4},{16,24},{20,12},{24,0},{28,20},{1,9},{5... | collective-permute-start | bytes 1327112 | tf_op jit(solution)/shard_map/ppermute | solution.py:568
  46.8 17.4 %collective-permute-start.9 = (f32[72,384]{1,0:T(8,128)S(1)}, f32[72,384]{1,0:T(8,128)S(1)}, u32[]{:S(2)}, u32[]{:S(2)}) collective-permute-start(f32[72,384]{1,0:T(8,128)S(1)} %get-tuple-element.32), channel_id=1, source_target_pairs={{4,8},{8,4},{12,16},{16,12},{20,24},{24,20},{28,0},{0,28},{5,9},{9... | collective-permute-start | bytes 331784 | tf_op jit(solution)/shard_map/ppermute | solution.py:568
  48.5 15.7 %collective-permute-start.8 = (f32[72,384]{1,0:T(8,128)S(1)}, f32[72,384]{1,0:T(8,128)S(1)}, u32[]{:S(2)}, u32[]{:S(2)}) collective-permute-start(f32[72,384]{1,0:T(8,128)S(1)} %get-tuple-element.32), channel_id=1, source_target_pairs={{0,4},{4,0},{8,12},{12,8},{16,20},{20,16},{24,28},{28,24},{1,5},{5... | collective-permute-start | bytes 331784 | tf_op jit(solution)/shard_map/ppermute | solution.py:568
  64.3 5.2 %copy-start.1 = (f32[3,3,48,384]{3,2,1,0:T(8,128)S(1)}, f32[3,3,48,384]{3,2,1,0:T(8,128)}, u32[]{:S(2)}) copy-start(f32[3,3,48,384]{3,2,1,0:T(8,128)} %g.7) | copy-start | bytes 1990660
  80.7 5.6 %collective-permute-start.13 = (f32[192,128]{1,0:T(8,128)S(1)}, f32[192,128]{1,0:T(8,128)S(1)}, u32[]{:S(2)}, u32[]{:S(2)}) collective-permute-start(f32[192,128]{1,0:T(8,128)S(1)} %get-tuple-element.46), channel_id=1, source_target_pairs={{0,4},{4,0},{8,12},{12,8},{16,20},{20,16},{24,28},{28,24},{1,5},{5... | collective-permute-start | bytes 294920 | tf_op jit(solution)/shard_map/ppermute | solution.py:568
  81.3 7.5 %collective-permute-start.14 = (f32[192,128]{1,0:T(8,128)S(1)}, f32[192,128]{1,0:T(8,128)S(1)}, u32[]{:S(2)}, u32[]{:S(2)}) collective-permute-start(f32[192,128]{1,0:T(8,128)S(1)} %get-tuple-element.47), channel_id=1, source_target_pairs={{4,8},{8,4},{12,16},{16,12},{20,24},{24,20},{5,9},{9,5},{13,17},{1... | collective-permute-start | bytes 294920 | tf_op jit(solution)/shard_map/ppermute | solution.py:568

commit v2 on v1

--- a/solution.py
+++ b/solution.py
@@ -13,7 +13,6 @@
 COARSE_SWEEPS = 8
 DEEP = 3
 O = 16
-LO = 8
 WIDTH_TABLE = (2.5, 3.5, 4.5, 5.0, 6.0, 7.0, 8.5, 10.0)
 RELAXATION = 0.8
 COARSE_RELAX = 0.8
@@ -32,7 +31,7 @@
     return n * (-(-shape[-2] // 8) * 8) * (-(-shape[-1] // BLOCK) * BLOCK)
 
 
-def call(kernel, outs, scratch, *args, smem=0, alias=None, cost=(1000000, 1000000)):
+def call(kernel, outs, scratch, *args, smem=0, cost=(1000000, 1000000)):
     specs = [SM] * smem + [VM] * (len(args) - smem)
     need = sum(map(padded, scratch))
     return pl.pallas_call(
@@ -41,7 +40,6 @@
         in_specs=specs,
         out_specs=[VM] * len(outs),
         scratch_shapes=[pltpu.VMEM(s, F32) for s in scratch],
-        input_output_aliases=alias or {},
         cost_estimate=pl.CostEstimate(flops=cost[0], bytes_accessed=cost[1], transcendentals=0),
         compiler_params=pltpu.CompilerParams(vmem_limit_bytes=need + (6 << 20)),
     )(*args)
@@ -63,7 +61,7 @@
                 to_b[at:at + DEEP, :] = jnp.where(even, first, last)
 
 
-def pack_k(info, a_in, b_in, ks, kp, ko, ka, kb, to_a, to_b, cols, *, nf, nz, nb):
+def pack_k(info, ks, kp, ko, ka, kb, to_a, to_b, cols, *, nz, nb):
     nx = ks.shape[0]
     n = nz * nb
     lane = iota((nx, BLOCK), 1)
@@ -84,14 +82,9 @@
     kall = kall + shift(only(hi1, 0, n, info[2]), nb + 2 * n) + shift(only(hi2, 0, nb, info[9]), nb + 3 * n)
     cols[...] = kall
     even = info[6] == 0
-    kr = kappa_row(nf, nz)
-    first, last = kall[0:4, :], kall[nx - 4:nx, :]
-    to_a[kr:kr + 4, 0:BLOCK] = jnp.where(even, last, first)
-    to_b[kr:kr + 4, 0:BLOCK] = jnp.where(even, first, last)
-
-
-def kappa_row(nf, nz):
-    return -(-2 * nf * nz * DEEP // 8) * 8
+    first, last = kall[0:8, :], kall[nx - 8:nx, :]
+    to_a[...] = jnp.where(even, last, first)
+    to_b[...] = jnp.where(even, first, last)
 
 
 def pack_y(info, xa, xb, out, low, high, *, nf, nz):
@@ -159,7 +152,7 @@
 
 
 def rows_of(wide, nx):
-    return range(LO, LO + nx + 16, 8) if wide else range(O, O + nx, 8)
+    return range(O - 4, O + nx + 4, 8) if wide else range(O, O + nx, 8)
 
 
 def sweep(dst, src, rhs, coef, first, count, stride, wide, nx):
@@ -181,19 +174,23 @@
     lax.fori_loop(0, count, plane, 0)
 
 
-def three(ua, ub, rhs, coef, nz, nx):
-    sweep(ub, ua, rhs, coef, 2, 2 * nz - 1, 1, True, nx)
+def three(ua, ub, rhs, coef, nz, nx, ahead=False):
+    if ahead:
+        sweep(ub, ua, rhs, coef, 2, 2, 1, True, nx)
+        sweep(ub, ua, rhs, coef, 2 * nz - 1, 2, 1, True, nx)
+    else:
+        sweep(ub, ua, rhs, coef, 2, 2 * nz - 1, 1, True, nx)
     sweep(ub, ua, rhs, coef, 1, 2, 3 * nz - 3, False, nx)
     sweep(ua, ub, rhs, coef, nz, nz, 1, True, nx)
     sweep(ua, ub, rhs, coef, nz - 1, 2, nz + 1, False, nx)
 
 
-def final(dst, src, rhs, coef, nz, nx):
+def final(dst, src, rhs, coef, nz, nx, which):
     inv = coef[4]
     nf, nb = src.shape[0], src.shape[2]
     lane = iota((8, BLOCK), 1)
 
-    def plane(i, _):
+    def plane(i):
         p = nz + i
         for r in rows_of(False, nx):
             co = coefs_at(coef, p, r, nb)
@@ -206,7 +203,8 @@
                     dst[a, i, q:q + 8, c] = (1.0 - RELAXATION) * v[b] + w[b] * (rhs[a, i, q:q + 8, c] + s[b])
         return 0
 
-    lax.fori_loop(0, nz, plane, 0)
+    for i in which:
+        plane(i)
 
 
 def restrict_residual(out, base, src, rhs, coef, diag, tmp, parts, nz, nx):
@@ -217,7 +215,7 @@
         p = nz + i
         for r in rows_of(False, nx):
             co = coefs_at(coef, p, r, nb)
-            d = [diag[i, b, r:r + 8, :] for b in range(nb)]
+            d = [diag[p, b, r:r + 8, :] for b in range(nb)]
             for a in range(nf):
                 v, s = pull(src, co, p, r, a, nb, lane)
                 for b in range(nb):
@@ -248,10 +246,11 @@
         out[rows, :] = out[rows, :] + dot01(kc, pick)
 
 
-def coefficients(info, cols, low, high, cz, cx, cm, cp, inv, diag, kap, *, nz, nx, nb, at):
+def coefficients(info, cols, xa, xb, cz, cx, cm, cp, inv, diag, kap, *, nz, nx, nb):
     first_j, last_j, first_g, last_g = (info[i] for i in range(1, 5))
-    below = jnp.where(first_g == 1, 0.0, low[at:at + 4, 0:BLOCK])
-    above = jnp.where(last_g == 1, 0.0, high[at:at + 4, 0:BLOCK])
+    even = info[6] == 0
+    below = jnp.where(first_g == 1, 0.0, jnp.where(even, xb[4:8, :], xa[4:8, :]))
+    above = jnp.where(last_g == 1, 0.0, jnp.where(even, xa[0:4, :], xb[0:4, :]))
     for row, value in ((O - 4, below), (O, cols[...]), (O + nx, above)):
         n = value.shape[0]
         for p in range(3 * nz + 2):
@@ -268,33 +267,27 @@
             s8 = slice(r, r + 8)
             k = [kap[p + 1, b, s8, :] for b in range(nb)]
             for b in range(nb):
-                zm = 0.5 * (kap[p, b, s8, :] + k[b])
-                zp = 0.5 * (k[b] + kap[p + 2, b, s8, :])
-                xp = 0.5 * (k[b] + kap[p + 1, b, r + 1:r + 9, :])
-                xm = 0.5 * (k[b] + kap[p + 1, b, r - 1:r + 7, :])
+                below, above = kap[p, b, s8, :], kap[p + 2, b, s8, :]
+                before, behind = kap[p + 1, b, r - 1:r + 7, :], kap[p + 1, b, r + 1:r + 9, :]
                 ym = jnp.where(lane == 0, 0.5 * (k[b] + k[b - 1]) if b > 0 else 0.5 * k[b], k[b])
                 yp = jnp.where(lane == BLOCK - 1, 0.5 * (k[b] + k[b + 1]) if b < nb - 1 else 0.5 * k[b], k[b])
-                cz[p, b, s8, :] = zm
-                cz[p + 1, b, s8, :] = zp
-                cx[p, b, s8, :] = xp
+                cz[p, b, s8, :] = 0.5 * (below + k[b])
+                cx[p, b, s8, :] = 0.5 * (k[b] + behind)
                 cm[p, b, s8, :] = ym
                 cp[p, b, s8, :] = yp
-                d = 1.0 + zm + zp + xm + xp + ym + yp
+                d = (1.0 + 2.0 * k[b]) + 0.5 * ((below + above) + (before + behind)) + (ym + yp)
                 inv[p, b, s8, :] = here / d
-
-                @pl.when((p >= nz) & (p < 2 * nz))
-                def _():
-                    diag[p - nz, b, s8, :] = d
+                diag[p, b, s8, :] = d
         return 0
 
     lax.fori_loop(0, 3 * nz, cplane, 0)
 
 
-def lay(dst, ref, a, p, q, rows, lo_row, hi_row, nx, nb):
+def lay(dst, ref, a, p, q, rows, lo_row, hi_row, nx, nb, field=None):
     width, _, pack = rows
     for b in range(nb):
         c = slice(b * BLOCK, (b + 1) * BLOCK)
-        dst[a, q, b, O:O + nx, :] = ref[a, p, :, c]
+        dst[a, q, b, O:O + nx, :] = ref[a if field is None else field, p, :, c]
         if pack is not None:
             dst[a, q, b, O - width:O, :] = pack[0][lo_row:lo_row + width, c]
             dst[a, q, b, O + nx:O + nx + width, :] = pack[1][hi_row:hi_row + width, c]
@@ -317,7 +310,7 @@
                 dst[a, p, b, r:r + 8, :] = inv[p, b, r:r + 8, :] * own[a, p, b, r:r + 8, :]
 
 
-def fwd_before(info, f, pf, rf, low, high, py, ry, ks, cz, cx, cm, cp, inv, diag, u3, rc, fx, ub, tmp, parts):
+def fwd_before(info, f, pfa, pfb, rfa, rfb, low, high, py, ry, ks, cz, cx, cm, cp, inv, diag, u3, rc, fx, ub, tmp, parts):
     nf, nz, nx, ny = f.shape
     nb = ny // BLOCK
     par = info[0]
@@ -326,8 +319,9 @@
     for a in range(nf):
         for p in range(nz):
             lay(fx, f, a, p, nz + p, *ends(low, high, 0, a, p, nf, nz), nx, nb)
-            lay(fx, pf, a, p, pbase + p, *corners(py, 0, a, p, nf, nz), nx, nb)
-            lay(fx, rf, a, p, rbase + p, *corners(ry, 0, a, p, nf, nz), nx, nb)
+            pf, rf, at = (pfa, rfa, a) if a < nf - 1 else (pfb, rfb, 0)
+            lay(fx, pf, a, p, pbase + p, *corners(py, 0, a, p, nf, nz), nx, nb, at)
+            lay(fx, rf, a, p, rbase + p, *corners(ry, 0, a, p, nf, nz), nx, nb, at)
     coef = (cz, cx, cm, cp, inv)
 
     def one(p, _):
@@ -340,18 +334,17 @@
     coarse_kappa(rc, ks, tmp, nz, nx, nb)
 
 
-def adj_before(info, g, pg, rn, low, high, rcf, cz, cx, cm, cp, inv, diag, rc, gx, ua, tmp, parts):
+def adj_before(info, g, pgn, rn, low, high, rcf, cz, cx, cm, cp, inv, diag, rc, gx, ua, tmp, parts):
     nf, nz, nx, ny = g.shape
     nb = ny // BLOCK
     par = info[0]
     pp = jnp.where(par == 0, 2 * nz, nz - 1)
     rp = 3 * nz - 1 - pp
-    near = jnp.where(par == 0, 0, nz - 1)
     none = (0, None, None)
     for a in range(nf):
         for p in range(nz):
             lay(gx, g, a, p, nz + p, *ends(low, high, 1, a, p, nf, nz), nx, nb)
-        lay(gx, pg, a, near, pp, none, 0, 0, nx, nb)
+        lay(gx, pgn, a, par, pp, none, 0, 0, nx, nb)
         lay(gx, rn, a, 0, rp, none, 0, 0, nx, nb)
 
     def one(p, _):
@@ -372,21 +365,37 @@
             dst[a, q, b, pl.ds(O - 4 + j, nc + 2, stride=4), :] = part
 
 
-def middle(info, u3, g, pg, rn, rr, low, high, py, ry, inv, est, uf, gx, ug, tmp, e):
+def add_rows(dst, src, other, p, q, nx):
+    for a in range(src.shape[0]):
+        for b in range(src.shape[2]):
+            for r in rows_of(True, nx):
+                dst[a, p, b, r:r + 8, :] = src[a, p, b, r:r + 8, :] + other[a, q, b, r:r + 8, :]
+
+
+def copy_rows(dst, src, p, nx):
+    for a in range(src.shape[0]):
+        for b in range(src.shape[2]):
+            for r in rows_of(True, nx):
+                dst[a, p, b, r:r + 8, :] = src[a, p, b, r:r + 8, :]
+
+
+def middle(info, u3, f, g, pgn, pgm, rn, rr, rm, low, high, py, ry, cz, cx, cm, cp, inv, est, uf, gx, ug, ub, filtered, tmp, e):
     nf, nz, nx, ny = g.shape
     nb = ny // BLOCK
     par = info[0]
     pbase = jnp.where(par == 0, 2 * nz, 0)
     rbase = 2 * nz - pbase
     near = jnp.where(par == 0, nz - 1, 0)
-    rest = jnp.where(par == 0, 0, 1)
+    none = (0, None, None)
     for a in range(nf):
         for p in range(nz):
             lay(gx, g, a, p, nz + p, *ends(low, high, 1, a, p, nf, nz), nx, nb)
-            lay(gx, pg, a, p, pbase + p, *corners(py, 1, a, p, nf, nz), nx, nb)
-        lay(gx, rn, a, 0, rbase + near, (0, None, None), 0, 0, nx, nb)
-        for p in range(nz - 1):
-            lay(gx, rr, a, p, rbase + rest + p, (0, None, None), 0, 0, nx, nb)
+            ref, at = (pgm, p - 1) if 0 < p < nz - 1 else (pgn, min(p, 1))
+            lay(gx, ref, a, at, pbase + p, *corners(py, 1, a, p, nf, nz), nx, nb)
+        lay(gx, rn, a, 0, rbase + near, none, 0, 0, nx, nb)
+        lay(gx, rr, a, 0, rbase + nz - 1 - near, none, 0, 0, nx, nb)
+        for p in range(1, nz - 1):
+            lay(gx, rm, a, p - 1, rbase + p, none, 0, 0, nx, nb)
         for p in range(nz):
             (width, _, pack), lo_row, hi_row = corners(ry, 1, a, p, nf, nz)
             for b in range(nb):
@@ -400,50 +409,44 @@
 
     lax.fori_loop(0, 3 * nz, one, 0)
     e[...] = dot01(est[...], lane_copy(ny))
-    for s, dst in enumerate((uf, ug)):
+    for s, (dst, src) in enumerate(((uf, u3), (ug, ug))):
         for a in range(nf):
             for i in range(nz):
                 prolong(tmp, e, (s * nf + a) * nz + i, a, i, nx, nb)
-
-        def add(i, _):
-            for a in range(nf):
-                for b in range(nb):
-                    for r in rows_of(True, nx):
-                        dst[a, nz + i, b, r:r + 8, :] = dst[a, nz + i, b, r:r + 8, :] + tmp[a, i, b, r:r + 8, :]
-            return 0
-
-        lax.fori_loop(0, nz, add, 0)
-
-
-def last(info, f, g, gx, uf_in, ug_in, cz, cx, cm, cp, inv, ea, eb, filtered, adjoint, uf, ug, ub, e):
+        for i in range(nz):
+            add_rows(dst, src, tmp, nz + i, i, nx)
+    for p in (nz - 1, 2 * nz):
+        copy_rows(uf, u3, p, nx)
+    coef = (cz, cx, cm, cp, inv)
+    final(filtered, uf, f, coef, nz, nx, range(1, nz - 1))
+    sweep(ub, ug, gx, coef, nz + 1, nz - 2, 1, True, nx)
+
+
+def last(info, f, g, gx, uf_in, ug_in, ub_in, filtered_in, cz, cx, cm, cp, inv, ea, eb, filtered, adjoint, uf, ug, ub, tmp, e):
     nf, nz, nx, ny = f.shape
     nb = ny // BLOCK
     coef = (cz, cx, cm, cp, inv)
     pbase = jnp.where(info[0] == 0, 2 * nz, 0)
     copy = lane_copy(ny)
     edge = jnp.where(info[0] == 0, 2 * nz, nz - 1)
+    for p in range(nz, 2 * nz):
+        copy_rows(uf, uf_in, p, nx)
+        copy_rows(ug, ug_in, p, nx)
+    for p in range(nz + 1, 2 * nz - 1):
+        copy_rows(ub, ub_in, p, nx)
+        filtered[:, p - nz, :, :] = filtered_in[:, p - nz, :, :]
     for ref, base, q in ((ea, pbase, edge), (eb, 2 * nz - pbase, 3 * nz - 1 - edge)):
         e[...] = dot01(ref[...], copy)
         for a in range(nf):
-            prolong(ub, e, a, a, 0, nx, nb)
+            prolong(tmp, e, a, a, 0, nx, nb)
             for i in range(nz):
-                prolong(ub, e, nf + a * nz + i, a, 1 + i, nx, nb)
-        for a in range(nf):
-            for b in range(nb):
-                for r in rows_of(True, nx):
-                    uf[a, q, b, r:r + 8, :] = uf[a, q, b, r:r + 8, :] + ub[a, 0, b, r:r + 8, :]
-
-        def add(i, _):
-            for a in range(nf):
-                for b in range(nb):
-                    for r in rows_of(True, nx):
-                        ug[a, base + i, b, r:r + 8, :] = ug[a, base + i, b, r:r + 8, :] + ub[a, 1 + i, b, r:r + 8, :]
-            return 0
-
-        lax.fori_loop(0, nz, add, 0)
-    final(filtered, uf, f, coef, nz, nx)
-    three(ug, ub, gx, coef, nz, nx)
-    final(adjoint, ug, g, coef, nz, nx)
+                prolong(tmp, e, nf + a * nz + i, a, 1 + i, nx, nb)
+        add_rows(uf, uf_in, tmp, q, 0, nx)
+        for i in range(nz):
+            add_rows(ug, ug_in, tmp, base + i, 1 + i, nx)
+    final(filtered, uf, f, coef, nz, nx, (0, nz - 1))
+    three(ug, ub, gx, coef, nz, nx, True)
+    final(adjoint, ug, g, coef, nz, nx, range(nz))
 
 
 def coarse(info, rc, est, to_a, to_b, full, e0, e1, ck, cf, *, nf, nz, ng, nc, nb):
@@ -546,7 +549,7 @@
     nb = ny // BLOCK
     nc = nx // 4
     nj, ng = lax.axis_size("jet"), lax.axis_size("grp")
-    assert nz == DEEP and nj % 4 == 0 and ng % 2 == 0
+    assert nz == DEEP and nj % 4 == 0 and ng % 4 == 0 and ng & (ng - 1) == 0
     j, gi = lax.axis_index("jet"), lax.axis_index("grp")
     par = j % 2
     zp = (j // 2) % 2
@@ -567,37 +570,39 @@
     def send(x, axis, perm):
         return lax.ppermute(x, axis, perm)
 
-    pf = send(f, "jet", swap)
+    pfa, pfb = send(f[:nf - 1], "jet", swap), send(f[nf - 1:], "jet", swap)
     ks = kappa_columns(width_class)
     near_k = [send(ks, "jet", swap), send(ks, "jet", side), send(ks, "jet", two_a), send(ks, "jet", two_b)]
-    xs = (kappa_row(nf, nz) + 8, ny)
+    xs = (-(-2 * nf * nz * DEEP // 8) * 8, ny)
     to_a, to_b = call(pack_x, [xs, xs], [], info, f, g, smem=1)
-    to_a, to_b, cols = call(
-        functools.partial(pack_k, nf=nf, nz=nz, nb=nb), [xs, xs, (nx, BLOCK)], [],
-        info, to_a, to_b, ks, *near_k, smem=1, alias={1: 0, 2: 1})
     xa, xb = send(to_a, "grp", x_a), send(to_b, "grp", x_b)
     ypack, low, high = call(functools.partial(pack_y, nf=nf, nz=nz), [(8 * nf * nz, ny), xs, xs], [], info, xa, xb, smem=1)
     py = send(ypack, "jet", swap)
     ry = send(ypack, "jet", side)
-    pg = send(g, "jet", swap)
-    rf = send(pf, "jet", relay)
-    near = lax.dynamic_slice_in_dim(pg, (1 - par) * (nz - 1), 1, 1)
-    rest = lax.dynamic_slice_in_dim(pg, par, nz - 1, 1)
+    outer = jnp.concatenate([g[:, :1], g[:, nz - 1:]], axis=1)
+    mids = g[:, 1:nz - 1]
+    pgn, pgm = send(outer, "jet", swap), send(mids, "jet", swap)
+    k_to_a, k_to_b, cols = call(
+        functools.partial(pack_k, nz=nz, nb=nb), [(8, BLOCK), (8, BLOCK), (nx, BLOCK)], [], info, ks, *near_k, smem=1)
+    kxa, kxb = send(k_to_a, "grp", x_a), send(k_to_b, "grp", x_b)
+    rfa, rfb = send(pfa, "jet", relay), send(pfb, "jet", relay)
+    near = lax.dynamic_slice_in_dim(pgn, 1 - par, 1, 1)
+    rest = lax.dynamic_slice_in_dim(pgn, par, 1, 1)
     rn = send(near, "jet", relay)
-    rr = send(rest, "jet", relay)
+    rr, rm = send(rest, "jet", relay), send(pgm, "jet", relay)
 
     xr = nx + 32
     deep = (nf, 3 * nz, nb, xr, BLOCK)
     co = (3 * nz, nb, xr, BLOCK)
     coefs = call(
-        functools.partial(coefficients, nz=nz, nx=nx, nb=nb, at=kappa_row(nf, nz)),
-        [(3 * nz + 1, nb, xr, BLOCK), co, co, co, co, (nz, nb, xr, BLOCK)], [(3 * nz + 2, nb, xr, BLOCK)],
-        info, cols, low, high, smem=1)
+        functools.partial(coefficients, nz=nz, nx=nx, nb=nb),
+        [co] * 6, [(3 * nz + 2, nb, xr, BLOCK)],
+        info, cols, kxa, kxb, smem=1)
     coef, diag = coefs[:5], coefs[5]
     rows = -(-nf * nz * nc // 8) * 8
     scratch = [(nb, nf * nz, nx, BLOCK), (rows, BLOCK)]
-    u3, rcf = call(fwd_before, [deep, (rows, BLOCK)], [deep, deep] + scratch, info, f, pf, rf, low, high, py, ry, ks, *coef, diag, smem=1)
-    (rc,) = call(adj_before, [(2 * rows, BLOCK)], [deep, deep] + scratch, info, g, pg, rn, low, high, rcf, *coef, diag, smem=1)
+    u3, rcf = call(fwd_before, [deep, (rows, BLOCK)], [deep, deep] + scratch, info, f, pfa, pfb, rfa, rfb, low, high, py, ry, ks, *coef, diag, smem=1)
+    (rc,) = call(adj_before, [(2 * rows, BLOCK)], [deep, deep] + scratch, info, g, pgn, rn, low, high, rcf, *coef, diag, smem=1)
     whole = lax.all_gather(rc, "grp", axis=0, tiled=True)
     nr = ng * nc
     solve = [(2 * nf * nz, nr, BLOCK), (2 * nf, nr + 16, BLOCK), (2 * nf, nr + 16, BLOCK), (nz, nr + 16, BLOCK), (5, nr, BLOCK)]
@@ -606,12 +611,12 @@
         functools.partial(coarse, nf=nf, nz=nz, ng=ng, nc=nc, nb=nb),
         [(2 * nf * nz * 16, BLOCK), sent, sent], solve, info, whole, smem=1)
     ea, eb = send(to_a, "jet", swap), send(to_b, "jet", inner)
-    uf, gx, ug = call(
-        middle, [deep] * 3, [deep, (2 * nf * nz * 16, ny)],
-        info, u3, g, pg, rn, rr, low, high, py, ry, coef[4], est, smem=1, alias={1: 0})
-    filtered, adjoint, _, _ = call(
-        last, [f.shape, g.shape, deep, deep], [deep, (nf * (nz + 1) * 16, ny)],
-        info, f, g, gx, uf, ug, *coef, ea, eb, smem=1, alias={4: 2, 5: 3})
+    uf, gx, ug, ub, done = call(
+        middle, [deep] * 4 + [f.shape], [(nf, nz, nb, xr, BLOCK), (2 * nf * nz * 16, ny)],
+        info, u3, f, g, pgn, pgm, rn, rr, rm, low, high, py, ry, *coef, est, smem=1)
+    filtered, adjoint = call(
+        last, [f.shape, g.shape], [deep] * 3 + [(nf, nz + 1, nb, xr, BLOCK), (nf * (nz + 1) * 16, ny)],
+        info, f, g, gx, uf, ug, ub, done, *coef, ea, eb, smem=1)
     return filtered, adjoint
 
 

time: 96.5 us -> 94.2 us (0.976)
  starting transfers between devices: 21.7 us -> 46.1 us
  waiting for transfers between devices: 38.8 us -> 16.4 us
  Pallas kernels: 24.8 us -> 20.6 us
    ppermute x15 -> x21, starting transfers between devices: 21.7 us -> 46.1 us  [send(): return lax.ppermute(x, axis, perm)]
    ppermute x15 -> x21, waiting for transfers between devices: 38.8 us -> 16.4 us  [send(): return lax.ppermute(x, axis, perm)]
    pallas_call x9, Pallas kernels: 24.8 us -> 20.6 us  [call(): pl.pallas_call(kernel, out_shape=[jax.ShapeDtypeStruct(s, F32) for s in o...]
    unnamed x8, local copies, waits for them, and re-layouts: 2.19 us -> 0.02 us
    slice x0 -> x3, local copies, waits for them, and re-layouts: none -> 1.86 us  [the longest x2 1.12 us: cycle(): pfa, pfb = (send(f[:nf - 1], 'jet', swap), send(f[nf - 1:], 'jet', swap))]
  transfers between devices with their start and end apart: 15 -> 21, of which waited for: 5 -> 5; matrix products, arithmetic and copies ran while one was open for 1% -> 2% of each run, Pallas kernels for 18% -> 16%
where the time goes in v2:
time: 94.2 us; the launch traced here: 93.5 us
  starting transfers between devices  46.1 us (49%)
  Pallas kernels  20.6 us (22%)
  waiting for transfers between devices  16.4 us (17%)
  blocking collectives  6.61 us (7%)
  local copies, waits for them, and re-layouts  2.11 us (2%)
    ppermute x21, starting transfers between devices, send(): return lax.ppermute(x, axis, perm)  46.1 us
    pallas_call x9, Pallas kernels, call(): pl.pallas_call(kernel, out_shape=[jax.ShapeDtypeStruct(s, F32) for s in o...  20.6 us
    ppermute x21, waiting for transfers between devices, send(): return lax.ppermute(x, axis, perm)  16.4 us
    all_gather x1, blocking collectives, cycle(): whole = lax.all_gather(rc, 'grp', axis=0, tiled=True)  6.61 us
  transfers between devices with their start and end apart: 21, of which 5 were waited for; matrix products, arithmetic and copies ran while one was open for 2% of the time, Pallas kernels for 16%

profile of v2, /device:TPU:4, one launch (start us, length us, event | category | flops | bytes accessed | tf_op | source)
XLA Modules:
  0.0 93.5 jit_solution(8028656814673792282)
XLA Ops:
  0.6 0.0 copy-start.1
  0.6 1.1 %slice.15 = f32[2,3,48,384]{3,2,1,0:T(8,128)S(1)} slice(f32[3,3,48,384]{3,2,1,0:T(8,128)} %f.7), slice={[0:2], [0:3], [0:48], [0:384]} | slice | bytes 884736 | tf_op jit(solution)/shard_map/slice | solution.py:573
  1.8 0.0 copy-start
  1.8 0.0 copy-start.2
  1.8 0.0 copy-start.3
  1.8 0.1 collective-permute-start
  1.9 0.0 copy-done.1
  1.9 0.7 fusion
  2.6 0.8 pad_maximum_fusion
  3.4 2.0 %collective-permute-start.14 = (f32[3,2,48,384]{3,2,1,0:T(8,128)}, f32[3,2,48,384]{3,2,1,0:T(8,128)S(1)}, u32[]{:S(2)}, u32[]{:S(2)}) collective-permute-start(f32[3,2,48,384]{3,2,1,0:T(8,128)} %pad_maximum_fusion), channel_id=1, source_target_pairs={{0,4},{4,0},{8,12},{12,8},{16,20},{20,16},{24,28},{28,24},{1,5},{5... | collective-permute-start | bytes 1327112 | tf_op jit(solution)/shard_map/ppermute | solution.py:571
  5.4 0.0 copy-done
  5.4 0.1 collective-permute-start.1
  5.5 0.1 select_reduce_fusion
  5.6 0.1 copy.9
  5.7 4.1 %collective-permute-start.11 = (f32[48,128]{1,0:T(8,128)S(1)}, f32[48,128]{1,0:T(8,128)S(1)}, u32[]{:S(2)}, u32[]{:S(2)}) collective-permute-start(f32[48,128]{1,0:T(8,128)S(1)} %pad.4.ks), channel_id=1, source_target_pairs={{8,16},{16,8},{12,20},{20,12},{24,0},{0,24},{28,4},{4,28},{9,17},{... | collective-permute-start | bytes 73736 | tf_op jit(solution)/shard_map/ppermute | solution.py:571
  9.9 0.0 collective-permute-start.10
  9.9 1.8 %collective-permute-done.11.kb = f32[48,128]{1,0:T(8,128)S(1)} collective-permute-done((f32[48,128]{1,0:T(8,128)S(1)}, f32[48,128]{1,0:T(8,128)S(1)}, u32[]{:S(2)}, u32[]{:S(2)}) %collective-permute-start.11) | collective-permute-done | bytes 24608 | tf_op jit(solution)/shard_map/ppermute | solution.py:571
  11.7 1.2 %collective-permute-start.9 = (f32[48,128]{1,0:T(8,128)S(1)}, f32[48,128]{1,0:T(8,128)S(1)}, u32[]{:S(2)}, u32[]{:S(2)}) collective-permute-start(f32[48,128]{1,0:T(8,128)S(1)} %pad.4.ks), channel_id=1, source_target_pairs={{4,8},{8,4},{12,16},{16,12},{20,24},{24,20},{28,0},{0,28},{5,9},{9... | collective-permute-start | bytes 73736 | tf_op jit(solution)/shard_map/ppermute | solution.py:571
  12.9 0.8 collective-permute-done.10.ka
  13.7 3.3 %collective-permute-start.8 = (f32[48,128]{1,0:T(8,128)S(1)}, f32[48,128]{1,0:T(8,128)S(1)}, u32[]{:S(2)}, u32[]{:S(2)}) collective-permute-start(f32[48,128]{1,0:T(8,128)S(1)} %pad.4.ks), channel_id=1, source_target_pairs={{0,4},{4,0},{8,12},{12,8},{16,20},{20,16},{24,28},{28,24},{1,5},{5... | collective-permute-start | bytes 73736 | tf_op jit(solution)/shard_map/ppermute | solution.py:571
  17.0 0.0 collective-permute-done.pfa
  17.0 1.5 %collective-permute-start.2 = (f32[2,3,48,384]{3,2,1,0:T(8,128)S(1)}, f32[2,3,48,384]{3,2,1,0:T(8,128)S(1)}, u32[]{:S(2)}, u32[]{:S(2)}) collective-permute-start(f32[2,3,48,384]{3,2,1,0:T(8,128)S(1)} %collective-permute-done.pfa), channel_id=1, source_target_pairs={{0,8},{4,28},{8,16},{12,4},{16,24},{20,12},{24,0},{28,20},{1,9},{5... | collective-permute-start | bytes 1327112 | tf_op jit(solution)/shard_map/ppermute | solution.py:571
  18.5 0.1 stack.67.info
  18.6 0.6 shard_map.59
  19.2 0.0 collective-permute-done.9.ko
  19.2 0.1 collective-permute-start.4
  19.3 9.8 %collective-permute-done.8.kp = f32[48,128]{1,0:T(8,128)S(1)} collective-permute-done((f32[48,128]{1,0:T(8,128)S(1)}, f32[48,128]{1,0:T(8,128)S(1)}, u32[]{:S(2)}, u32[]{:S(2)}) %collective-permute-start.8) | collective-permute-done | bytes 24608 | tf_op jit(solution)/shard_map/ppermute | solution.py:571
  29.0 0.1 collective-permute-start.5
  29.1 0.6 shard_map.61
  29.8 0.0 collective-permute-done.4.xa
  29.8 1.6 %collective-permute-start.12 = (f32[8,128]{1,0:T(8,128)S(1)}, f32[8,128]{1,0:T(8,128)S(1)}, u32[]{:S(2)}, u32[]{:S(2)}) collective-permute-start(f32[8,128]{1,0:T(8,128)S(1)} %get-tuple-element.32), channel_id=1, source_target_pairs={{0,1},{1,0},{2,3},{3,2},{4,5},{5,4},{6,7},{7,6},{8,9},{9,8},{10,11... | collective-permute-start | bytes 12296 | tf_op jit(solution)/shard_map/ppermute | solution.py:571
  31.4 2.5 %collective-permute-done.5.xb = f32[56,384]{1,0:T(8,128)S(1)} collective-permute-done((f32[56,384]{1,0:T(8,128)S(1)}, f32[56,384]{1,0:T(8,128)S(1)}, u32[]{:S(2)}, u32[]{:S(2)}) %collective-permute-start.5) | collective-permute-done | bytes 86048 | tf_op jit(solution)/shard_map/ppermute | solution.py:571
  33.8 0.1 collective-permute-start.15
  33.9 0.6 shard_map.60
  34.5 0.0 collective-permute-done.12.xa
  34.5 0.1 collective-permute-start.13
  34.6 0.0 collective-permute-done.1.pfb
  34.6 3.0 %collective-permute-start.7 = (f32[72,384]{1,0:T(8,128)S(1)}, f32[72,384]{1,0:T(8,128)S(1)}, u32[]{:S(2)}, u32[]{:S(2)}) collective-permute-start(f32[72,384]{1,0:T(8,128)S(1)} %get-tuple-element.30), channel_id=1, source_target_pairs={{4,8},{8,4},{12,16},{16,12},{20,24},{24,20},{28,0},{0,28},{5,9},{9... | collective-permute-start | bytes 331784 | tf_op jit(solution)/shard_map/ppermute | solution.py:571
  37.6 0.0 collective-permute-done.14.pgn
  37.6 2.2 %collective-permute-start.3 = (f32[1,3,48,384]{3,2,1,0:T(8,128)S(1)}, f32[1,3,48,384]{3,2,1,0:T(8,128)S(1)}, u32[]{:S(2)}, u32[]{:S(2)}) collective-permute-start(f32[1,3,48,384]{3,2,1,0:T(8,128)S(1)} %collective-permute-done.1.pfb), channel_id=1, source_target_pairs={{0,8},{4,28},{8,16},{12,4},{16,24},{20,12},{24,0},{28,20},{1,9},{5... | collective-permute-start | bytes 663560 | tf_op jit(solution)/shard_map/ppermute | solution.py:571
  39.9 0.0 collective-permute-done.13.xb
  39.9 1.9 %collective-permute-start.16 = (f32[3,1,48,384]{3,2,1,0:T(8,128)S(1)}, f32[3,1,48,384]{3,2,1,0:T(8,128)S(1)}, u32[]{:S(2)}, u32[]{:S(2)}) collective-permute-start(f32[3,1,48,384]{3,2,1,0:T(8,128)S(1)} %get-tuple-element.54), channel_id=1, source_target_pairs={{0,8},{4,28},{8,16},{12,4},{16,24},{20,12},{24,0},{28,20},{1,9},{5... | collective-permute-start | bytes 663560 | tf_op jit(solution)/shard_map/ppermute | solution.py:571
  41.8 0.0 collective-permute-done.7.ry
  41.8 3.5 %collective-permute-start.6 = (f32[72,384]{1,0:T(8,128)S(1)}, f32[72,384]{1,0:T(8,128)S(1)}, u32[]{:S(2)}, u32[]{:S(2)}) collective-permute-start(f32[72,384]{1,0:T(8,128)S(1)} %get-tuple-element.30), channel_id=1, source_target_pairs={{0,4},{4,0},{8,12},{12,8},{16,20},{20,16},{24,28},{28,24},{1,5},{5... | collective-permute-start | bytes 331784 | tf_op jit(solution)/shard_map/ppermute | solution.py:571
  45.3 1.6 %shard_map.62 = (f32[9,3,80,128]{3,2,1,0:T(8,128)S(1)}, f32[9,3,80,128]{3,2,1,0:T(8,128)S(1)}, f32[9,3,80,128]{3,2,1,0:T(8,128)S(1)}, f32[9,3,80,128]{3,2,1,0:T(...) custom-call(s32[10]{0:T(128)S(1)} %stack.67.info, f32[48,128]{1,0:T(8,128)S(1)} %get-tuple-element.31.cols, ...), custom_call_target="tpu_custom_call" | custom-call | flops 1000000 | bytes 1000000 | tf_op jit(solution)/shard_map/pallas_call | solution.py:37
  46.9 0.0 collective-permute-done.15.pgm
  46.9 15.9 %collective-permute-start.18 = (f32[3,1,48,384]{3,2,1,0:T(8,128)S(1)}, f32[3,1,48,384]{3,2,1,0:T(8,128)S(1)}, u32[]{:S(2)}, u32[]{:S(2)}) collective-permute-start(f32[3,1,48,384]{3,2,1,0:T(8,128)S(1)} %collective-permute-done.15.pgm), channel_id=1, source_target_pairs={{0,8},{4,28},{8,16},{12,4},{16,24},{20,12},{24,0},{28,20},{1,9},{5... | collective-permute-start | bytes 663560 | tf_op jit(solution)/shard_map/ppermute | solution.py:571
  62.7 0.0 collective-permute-done.6.py
  62.7 1.1 %collective-permute-start.17 = (f32[3,1,48,384]{3,2,1,0:T(8,128)S(1)}, f32[3,1,48,384]{3,2,1,0:T(8,128)S(1)}, u32[]{:S(2)}, u32[]{:S(2)}) collective-permute-start(f32[3,1,48,384]{3,2,1,0:T(8,128)S(1)} %get-tuple-element.53), channel_id=1, source_target_pairs={{0,8},{4,28},{8,16},{12,4},{16,24},{20,12},{24,0},{28,20},{1,9},{5... | collective-permute-start | bytes 663560 | tf_op jit(solution)/shard_map/ppermute | solution.py:571
  63.8 0.0 collective-permute-done.3.rfb
  63.8 0.0 collective-permute-done.2.rfa
  63.8 4.8 %shard_map.63 = (f32[3,9,3,80,128]{4,3,2,1,0:T(8,128)S(1)}, f32[112,128]{1,0:T(8,128)S(1)}) custom-call(s32[10]{0:T(128)S(1)} %stack.67.info, f32[3,3,48,384]{3,2,1,0:T(8,128)S(1)} %copy-done, f32[2,3,48,384]{3,2,1,0:T(8,128)S(1)} %collective-permute-done.pfa, f32[1,3,48,384]{3,2,1,0:T(8,128)S(1)} %collective-permute-done.1.pfb, ...), custom_call_target="tpu_custom_call" | custom-call | flops 1000000 | bytes 1000000 | tf_op jit(solution)/shard_map/pallas_call | solution.py:37
  68.6 0.0 collective-permute-done.16.rn
  68.7 1.7 %shard_map.64 = f32[224,128]{1,0:T(8,128)S(1)} custom-call(s32[10]{0:T(128)S(1)} %stack.67.info, f32[3,3,48,384]{3,2,1,0:T(8,128)S(1)} %copy-done.1, f32[3,2,48,384]{3,2,1,0:T(8,128)S(1)} %collective-permute-done.14.pgn, f32[3,1,48,384]{3,2,1,0:T(8,128)S(1)} %collective-permute-done.16.rn, f32[56,384]{1,0:T(8,128)S(1)} %get-tuple-element.28.low, ...), custom_call_target="tpu_custom_call" | custom-call | flops 1000000 | bytes 1000000 | tf_op jit(solution)/shard_map/pallas_call | solution.py:37
  70.4 6.6 %all_gather.3.rc = f32[896,128]{1,0:T(8,128)S(1)} all-gather(f32[224,128]{1,0:T(8,128)S(1)} %shard_map.64), channel_id=1, replica_groups=mesh['jet'=8,'grp'=4] {'grp'}, dimensions={0}, use_global_device_ids=true | all-gather | bytes 573440 | tf_op jit(solution)/shard_map/all_gather | solution.py:606
  77.0 2.9 %shard_map.65 = (f32[288,128]{1,0:T(8,128)S(1)}, f32[192,128]{1,0:T(8,128)S(1)}, f32[192,128]{1,0:T(8,128)S(1)}) custom-call(s32[10]{0:T(128)S(1)} %stack.67.info, f32[896,128]{1,0:T(8,128)S(1)} %all_gather.3.rc), custom_call_target="tpu_custom_call" | custom-call | flops 1000000 | bytes 1000000 | tf_op jit(solution)/shard_map/pallas_call | solution.py:37
  79.8 0.1 collective-permute-start.19
  79.9 4.3 %collective-permute-start.20 = (f32[192,128]{1,0:T(8,128)S(1)}, f32[192,128]{1,0:T(8,128)S(1)}, u32[]{:S(2)}, u32[]{:S(2)}) collective-permute-start(f32[192,128]{1,0:T(8,128)S(1)} %get-tuple-element.49), channel_id=1, source_target_pairs={{4,8},{8,4},{12,16},{16,12},{20,24},{24,20},{5,9},{9,5},{13,17},{1... | collective-permute-start | bytes 294920 | tf_op jit(solution)/shard_map/ppermute | solution.py:571
  84.2 0.0 collective-permute-done.18.rm
  84.2 0.0 collective-permute-done.17.rr
  84.3 2.0 %shard_map.66 = (f32[3,9,3,80,128]{4,3,2,1,0:T(8,128)S(1)}, f32[3,9,3,80,128]{4,3,2,1,0:T(8,128)S(1)}, f32[3,9,3,80,128]{4,3,2,1,0:T(8,128)S(1)}, f32[3,9,3,80,128]{4,3,2,1,0:T(8,128)S(1)}, f32[3,3,48,384]{3,2,1,0:T(8,128)S(1)}) custom-call(s32[10]{0:T(128)S(1)} %stack.67.info, f32[3,9,3,80,128]{4,3,2,1,0:T(8,128)S(1)} %get-tuple-element.40.u3, ...), custom_call_target="tpu_custom_call" | custom-call | flops 1000000 | bytes 1000000 | tf_op jit(solution)/shard_map/pallas_call | solution.py:37
  86.3 0.0 collective-permute-done.19.ea
  86.3 1.4 %collective-permute-done.20.eb = f32[192,128]{1,0:T(8,128)S(1)} collective-permute-done((f32[192,128]{1,0:T(8,128)S(1)}, f32[192,128]{1,0:T(8,128)S(1)}, u32[]{:S(2)}, u32[]{:S(2)}) %collective-permute-start.20) | collective-permute-done | bytes 98336 | tf_op jit(solution)/shard_map/ppermute | solution.py:571
  87.8 5.7 %shard_map.67 = (f32[3,3,48,384]{3,2,1,0:T(8,128)}, f32[3,3,48,384]{3,2,1,0:T(8,128)}) custom-call(s32[10]{0:T(128)S(1)} %stack.67.info, f32[3,3,48,384]{3,2,1,0:T(8,128)S(1)} %copy-done, f32[3,3,48,384]{3,2,1,0:T(8,128)S(1)} %copy-done.1, f32[3,9,3,80,128]{4,3,2,1,0:T(8,128)S(1)} %get-tuple-element.43.gx, ...), custom_call_target="tpu_custom_call" | custom-call | flops 1000000 | bytes 1000000 | tf_op jit(solution)/shard_map/pallas_call | solution.py:37
  (6 shorter events, 0.1 us)
Async XLA Ops:
  0.6 1.2 %copy-start.1 = (f32[3,3,48,384]{3,2,1,0:T(8,128)S(1)}, f32[3,3,48,384]{3,2,1,0:T(8,128)}, u32[]{:S(2)}) copy-start(f32[3,3,48,384]{3,2,1,0:T(8,128)} %g.7) | copy-start | bytes 1990660
  1.8 3.7 %copy-start = (f32[3,3,48,384]{3,2,1,0:T(8,128)S(1)}, f32[3,3,48,384]{3,2,1,0:T(8,128)}, u32[]{:S(2)}) copy-start(f32[3,3,48,384]{3,2,1,0:T(8,128)} %f.7) | copy-start | bytes 1990660
  1.8 3.8 %copy-start.2 = (s32[3,48,3]{1,2,0:T(4,128)S(1)}, s32[3,48,3]{1,2,0:T(4,128)}, u32[]{:S(2)}) copy-start(s32[3,48,3]{1,2,0:T(4,128)} %param.6) | copy-start | bytes 5188
  1.8 3.7 %copy-start.3 = (f32[8]{0:T(128)S(1)}, f32[8]{0:T(128)}, u32[]{:S(2)}) copy-start(f32[8]{0:T(128)} %constant.66) | copy-start | bytes 100
  1.8 15.2 %collective-permute-start = (f32[2,3,48,384]{3,2,1,0:T(8,128)S(1)}, f32[2,3,48,384]{3,2,1,0:T(8,128)S(1)}, u32[]{:S(2)}, u32[]{:S(2)}) collective-permute-start(f32[2,3,48,384]{3,2,1,0:T(8,128)S(1)} %slice.15), channel_id=1, source_target_pairs={{0,4},{4,0},{8,12},{12,8},{16,20},{20,16},{24,28},{28,24},{1,5},{5... | collective-permute-start | bytes 1327112 | tf_op jit(solution)/shard_map/ppermute | solution.py:571
  3.4 34.2 %collective-permute-start.14 = (f32[3,2,48,384]{3,2,1,0:T(8,128)}, f32[3,2,48,384]{3,2,1,0:T(8,128)S(1)}, u32[]{:S(2)}, u32[]{:S(2)}) collective-permute-start(f32[3,2,48,384]{3,2,1,0:T(8,128)} %pad_maximum_fusion), channel_id=1, source_target_pairs={{0,4},{4,0},{8,12},{12,8},{16,20},{20,16},{24,28},{28,24},{1,5},{5... | collective-permute-start | bytes 1327112 | tf_op jit(solution)/shard_map/ppermute | solution.py:571
  5.4 29.2 %collective-permute-start.1 = (f32[1,3,48,384]{3,2,1,0:T(8,128)S(1)}, f32[1,3,48,384]{3,2,1,0:T(8,128)S(1)}, u32[]{:S(2)}, u32[]{:S(2)}) collective-permute-start(f32[1,3,48,384]{3,2,1,0:T(8,128)S(1)} %slice.16), channel_id=1, source_target_pairs={{0,4},{4,0},{8,12},{12,8},{16,20},{20,16},{24,28},{28,24},{1,5},{5... | collective-permute-start | bytes 663560 | tf_op jit(solution)/shard_map/ppermute | solution.py:571
  5.7 6.0 %collective-permute-start.11 = (f32[48,128]{1,0:T(8,128)S(1)}, f32[48,128]{1,0:T(8,128)S(1)}, u32[]{:S(2)}, u32[]{:S(2)}) collective-permute-start(f32[48,128]{1,0:T(8,128)S(1)} %pad.4.ks), channel_id=1, source_target_pairs={{8,16},{16,8},{12,20},{20,12},{24,0},{0,24},{28,4},{4,28},{9,17},{... | collective-permute-start | bytes 73736 | tf_op jit(solution)/shard_map/ppermute | solution.py:571
  9.9 3.8 %collective-permute-start.10 = (f32[48,128]{1,0:T(8,128)S(1)}, f32[48,128]{1,0:T(8,128)S(1)}, u32[]{:S(2)}, u32[]{:S(2)}) collective-permute-start(f32[48,128]{1,0:T(8,128)S(1)} %pad.4.ks), channel_id=1, source_target_pairs={{0,8},{8,0},{4,12},{12,4},{16,24},{24,16},{20,28},{28,20},{1,9},{9... | collective-permute-start | bytes 73736 | tf_op jit(solution)/shard_map/ppermute | solution.py:571
  11.7 7.5 %collective-permute-start.9 = (f32[48,128]{1,0:T(8,128)S(1)}, f32[48,128]{1,0:T(8,128)S(1)}, u32[]{:S(2)}, u32[]{:S(2)}) collective-permute-start(f32[48,128]{1,0:T(8,128)S(1)} %pad.4.ks), channel_id=1, source_target_pairs={{4,8},{8,4},{12,16},{16,12},{20,24},{24,20},{28,0},{0,28},{5,9},{9... | collective-permute-start | bytes 73736 | tf_op jit(solution)/shard_map/ppermute | solution.py:571
  13.7 15.3 %collective-permute-start.8 = (f32[48,128]{1,0:T(8,128)S(1)}, f32[48,128]{1,0:T(8,128)S(1)}, u32[]{:S(2)}, u32[]{:S(2)}) collective-permute-start(f32[48,128]{1,0:T(8,128)S(1)} %pad.4.ks), channel_id=1, source_target_pairs={{0,4},{4,0},{8,12},{12,8},{16,20},{20,16},{24,28},{28,24},{1,5},{5... | collective-permute-start | bytes 73736 | tf_op jit(solution)/shard_map/ppermute | solution.py:571
  17.0 46.8 %collective-permute-start.2 = (f32[2,3,48,384]{3,2,1,0:T(8,128)S(1)}, f32[2,3,48,384]{3,2,1,0:T(8,128)S(1)}, u32[]{:S(2)}, u32[]{:S(2)}) collective-permute-start(f32[2,3,48,384]{3,2,1,0:T(8,128)S(1)} %collective-permute-done.pfa), channel_id=1, source_target_pairs={{0,8},{4,28},{8,16},{12,4},{16,24},{20,12},{24,0},{28,20},{1,9},{5... | collective-permute-start | bytes 1327112 | tf_op jit(solution)/shard_map/ppermute | solution.py:571
  19.2 10.6 %collective-permute-start.4 = (f32[56,384]{1,0:T(8,128)S(1)}, f32[56,384]{1,0:T(8,128)S(1)}, u32[]{:S(2)}, u32[]{:S(2)}) collective-permute-start(f32[56,384]{1,0:T(8,128)S(1)} %get-tuple-element.26), channel_id=1, source_target_pairs={{0,1},{1,0},{2,3},{3,2},{4,5},{5,4},{6,7},{7,6},{8,9},{9,8},{10,11... | collective-permute-start | bytes 258056 | tf_op jit(solution)/shard_map/ppermute | solution.py:571
  29.0 4.8 %collective-permute-start.5 = (f32[56,384]{1,0:T(8,128)S(1)}, f32[56,384]{1,0:T(8,128)S(1)}, u32[]{:S(2)}, u32[]{:S(2)}) collective-permute-start(f32[56,384]{1,0:T(8,128)S(1)} %get-tuple-element.27), channel_id=1, source_target_pairs={{1,2},{2,1},{3,0},{0,3},{5,6},{6,5},{7,4},{4,7},{9,10},{10,9},{11,... | collective-permute-start | bytes 258056 | tf_op jit(solution)/shard_map/ppermute | solution.py:571
  29.8 4.7 %collective-permute-start.12 = (f32[8,128]{1,0:T(8,128)S(1)}, f32[8,128]{1,0:T(8,128)S(1)}, u32[]{:S(2)}, u32[]{:S(2)}) collective-permute-start(f32[8,128]{1,0:T(8,128)S(1)} %get-tuple-element.32), channel_id=1, source_target_pairs={{0,1},{1,0},{2,3},{3,2},{4,5},{5,4},{6,7},{7,6},{8,9},{9,8},{10,11... | collective-permute-start | bytes 12296 | tf_op jit(solution)/shard_map/ppermute | solution.py:571
  33.8 13.0 %collective-permute-start.15 = (f32[3,1,48,384]{3,2,1,0:T(8,128)}, f32[3,1,48,384]{3,2,1,0:T(8,128)S(1)}, u32[]{:S(2)}, u32[]{:S(2)}) collective-permute-start(f32[3,1,48,384]{3,2,1,0:T(8,128)} %get-tuple-element.50), channel_id=1, source_target_pairs={{0,4},{4,0},{8,12},{12,8},{16,20},{20,16},{24,28},{28,24},{1,5},{5... | collective-permute-start | bytes 663560 | tf_op jit(solution)/shard_map/ppermute | solution.py:571
  34.5 5.4 %collective-permute-start.13 = (f32[8,128]{1,0:T(8,128)S(1)}, f32[8,128]{1,0:T(8,128)S(1)}, u32[]{:S(2)}, u32[]{:S(2)}) collective-permute-start(f32[8,128]{1,0:T(8,128)S(1)} %get-tuple-element.33), channel_id=1, source_target_pairs={{1,2},{2,1},{3,0},{0,3},{5,6},{6,5},{7,4},{4,7},{9,10},{10,9},{11,... | collective-permute-start | bytes 12296 | tf_op jit(solution)/shard_map/ppermute | solution.py:571
  34.6 7.2 %collective-permute-start.7 = (f32[72,384]{1,0:T(8,128)S(1)}, f32[72,384]{1,0:T(8,128)S(1)}, u32[]{:S(2)}, u32[]{:S(2)}) collective-permute-start(f32[72,384]{1,0:T(8,128)S(1)} %get-tuple-element.30), channel_id=1, source_target_pairs={{4,8},{8,4},{12,16},{16,12},{20,24},{24,20},{28,0},{0,28},{5,9},{9... | collective-permute-start | bytes 331784 | tf_op jit(solution)/shard_map/ppermute | solution.py:571
  37.6 26.2 %collective-permute-start.3 = (f32[1,3,48,384]{3,2,1,0:T(8,128)S(1)}, f32[1,3,48,384]{3,2,1,0:T(8,128)S(1)}, u32[]{:S(2)}, u32[]{:S(2)}) collective-permute-start(f32[1,3,48,384]{3,2,1,0:T(8,128)S(1)} %collective-permute-done.1.pfb), channel_id=1, source_target_pairs={{0,8},{4,28},{8,16},{12,4},{16,24},{20,12},{24,0},{28,20},{1,9},{5... | collective-permute-start | bytes 663560 | tf_op jit(solution)/shard_map/ppermute | solution.py:571
  39.9 28.7 %collective-permute-start.16 = (f32[3,1,48,384]{3,2,1,0:T(8,128)S(1)}, f32[3,1,48,384]{3,2,1,0:T(8,128)S(1)}, u32[]{:S(2)}, u32[]{:S(2)}) collective-permute-start(f32[3,1,48,384]{3,2,1,0:T(8,128)S(1)} %get-tuple-element.54), channel_id=1, source_target_pairs={{0,8},{4,28},{8,16},{12,4},{16,24},{20,12},{24,0},{28,20},{1,9},{5... | collective-permute-start | bytes 663560 | tf_op jit(solution)/shard_map/ppermute | solution.py:571
  41.8 20.9 %collective-permute-start.6 = (f32[72,384]{1,0:T(8,128)S(1)}, f32[72,384]{1,0:T(8,128)S(1)}, u32[]{:S(2)}, u32[]{:S(2)}) collective-permute-start(f32[72,384]{1,0:T(8,128)S(1)} %get-tuple-element.30), channel_id=1, source_target_pairs={{0,4},{4,0},{8,12},{12,8},{16,20},{20,16},{24,28},{28,24},{1,5},{5... | collective-permute-start | bytes 331784 | tf_op jit(solution)/shard_map/ppermute | solution.py:571
  46.9 37.4 %collective-permute-start.18 = (f32[3,1,48,384]{3,2,1,0:T(8,128)S(1)}, f32[3,1,48,384]{3,2,1,0:T(8,128)S(1)}, u32[]{:S(2)}, u32[]{:S(2)}) collective-permute-start(f32[3,1,48,384]{3,2,1,0:T(8,128)S(1)} %collective-permute-done.15.pgm), channel_id=1, source_target_pairs={{0,8},{4,28},{8,16},{12,4},{16,24},{20,12},{24,0},{28,20},{1,9},{5... | collective-permute-start | bytes 663560 | tf_op jit(solution)/shard_map/ppermute | solution.py:571
  62.7 21.5 %collective-permute-start.17 = (f32[3,1,48,384]{3,2,1,0:T(8,128)S(1)}, f32[3,1,48,384]{3,2,1,0:T(8,128)S(1)}, u32[]{:S(2)}, u32[]{:S(2)}) collective-permute-start(f32[3,1,48,384]{3,2,1,0:T(8,128)S(1)} %get-tuple-element.53), channel_id=1, source_target_pairs={{0,8},{4,28},{8,16},{12,4},{16,24},{20,12},{24,0},{28,20},{1,9},{5... | collective-permute-start | bytes 663560 | tf_op jit(solution)/shard_map/ppermute | solution.py:571
  79.8 6.5 %collective-permute-start.19 = (f32[192,128]{1,0:T(8,128)S(1)}, f32[192,128]{1,0:T(8,128)S(1)}, u32[]{:S(2)}, u32[]{:S(2)}) collective-permute-start(f32[192,128]{1,0:T(8,128)S(1)} %get-tuple-element.48), channel_id=1, source_target_pairs={{0,4},{4,0},{8,12},{12,8},{16,20},{20,16},{24,28},{28,24},{1,5},{5... | collective-permute-start | bytes 294920 | tf_op jit(solution)/shard_map/ppermute | solution.py:571
  79.9 7.8 %collective-permute-start.20 = (f32[192,128]{1,0:T(8,128)S(1)}, f32[192,128]{1,0:T(8,128)S(1)}, u32[]{:S(2)}, u32[]{:S(2)}) collective-permute-start(f32[192,128]{1,0:T(8,128)S(1)} %get-tuple-element.49), channel_id=1, source_target_pairs={{4,8},{8,4},{12,16},{16,12},{20,24},{24,20},{5,9},{9,5},{13,17},{1... | collective-permute-start | bytes 294920 | tf_op jit(solution)/shard_map/ppermute | solution.py:571
